TPU v7x, 512 devices: a whole 4x4x16 slice. The times are simulated.
512 devices in a mesh: section: 16 (over z), row: 8 (over y, core), col: 4 (over x).
Axes of the slice: x: 4, y: 4, z: 16, core: 2. Of those that a mesh axis runs over, the one named last changes fastest.
Arguments:
- x_fwd: bfloat16 [4096, 12288], P('section', 'row'), may hold values from -6 to 6
- dy_bwd: bfloat16 [4096, 12288], P(('section', 'row'), 'col'), may hold values from -6 to 6
- w_blocks: bfloat16 [16, 8, 4, 115, 128, 128], P('section', 'row', 'col'), may hold values from -0.09375 to 0.09375
- blk_row: int32 [16, 8, 4, 115], P('section', 'row', 'col'), may hold values from 0 to 11, as said below
- blk_col: int32 [16, 8, 4, 115], P('section', 'row', 'col'), may hold values from 0 to 23, as said below
- blk_count: int32 [16, 8, 4], P('section', 'row', 'col'), may hold values from 57 to 115, as said below
- tok_count: int32 [16, 2], P('section'), may hold values from 64 to 256, as said below
- owner_order: int32 [16, 64], P('section'), may hold values from 0 to 63, each once within a row
Outputs:
- y_next: bfloat16 [4096, 12288], P(('section', 'row', 'col'))
- dx_section: bfloat16 [4096, 12288], P(('section', 'row', 'col'))
Inputs may be any that keep to these rules, and one draw needn't show every extreme that they name: At each grid position the slots below blk_count name distinct block positions (blk_row, blk_col); the other slots name arbitrary positions. `blk_col`: see blk_row. `blk_count`: some grid position of every draw holds exactly 115 live slots. `tok_count`: index 0 counts the forward micro-batch, index 1 the backward one; valid tokens come first; some entry of every draw equals 256. `owner_order`: each section's row is a permutation.
All inputs are finite; a program needn't handle non-finite values.
Results may differ from a plain program's by a relative error of at most 0.015.
Values may be sent and summed in bfloat16 or wider, within the bound.
A program may use at most 128 MiB of HBM per device.

v0:
```python
import jax
import jax.numpy as jnp
from jax import lax
from jax.sharding import PartitionSpec as P


def passed_along(shard, axis, by):
    length = lax.axis_size(axis)
    pairs = [(i, i + by) for i in range(length) if 0 <= i + by < length]
    return lax.ppermute(shard, axis, pairs)


def local(x_fwd, dy_bwd, w_blocks, blk_row, blk_col, blk_count, tok_count, owner_order):
    row_count = lax.axis_size("row")
    col_count = lax.axis_size("col")
    token_total, in_width = x_fwd.shape
    out_width = dy_bwd.shape[1]
    slot_total = w_blocks.shape[3]
    block_size = w_blocks.shape[5]
    block_rows = in_width // block_size
    block_cols = out_width // block_size
    owned_rows = token_total // (row_count * col_count)
    weights = w_blocks.reshape(slot_total, block_size, block_size)
    live = (jnp.arange(slot_total) < blk_count.reshape(())).astype(weights.dtype)
    dense_blocks = jnp.zeros((block_rows, block_cols, block_size, block_size), weights.dtype)
    dense_blocks = dense_blocks.at[blk_row.reshape(slot_total), blk_col.reshape(slot_total)].add(
        weights * live[:, None, None]
    )
    dense_weight = jnp.transpose(dense_blocks, (0, 2, 1, 3)).reshape(in_width, out_width)
    limits = tok_count.reshape(2)
    block_total = owner_order.shape[1]
    block_length = token_total // block_total
    token_index = (
        owner_order.reshape(block_total)[:, None] * block_length + jnp.arange(block_length)[None, :]
    ).reshape(token_total)
    ordered_rows = jnp.take(x_fwd, token_index, axis=0)
    ordered_rows = jnp.where(
        (token_index < limits[0])[:, None], ordered_rows, jnp.zeros_like(ordered_rows)
    )
    partial_value = jnp.dot(ordered_rows, dense_weight, preferred_element_type=jnp.float32).astype(
        jnp.bfloat16
    )
    outgoing = partial_value.reshape(row_count * col_count, owned_rows, out_width)
    received = lax.all_to_all(outgoing, ("row", "col"), split_axis=0, concat_axis=2, tiled=True)
    summed = received.reshape(owned_rows, row_count, col_count * out_width).astype(jnp.float32)
    forward_act = jnp.sum(summed, axis=1).astype(jnp.bfloat16)
    y_next = passed_along(forward_act, "section", 1)
    grad_rows = dy_bwd.shape[0]
    grad_index = lax.axis_index("row") * grad_rows + jnp.arange(grad_rows)
    grad_kept = jnp.where((grad_index < limits[1])[:, None], dy_bwd, jnp.zeros_like(dy_bwd))
    grad_partial = lax.dot_general(
        lax.all_gather(grad_kept, "row", axis=0, tiled=True),
        dense_weight,
        (((1,), (1,)), ((), ())),
        preferred_element_type=jnp.float32,
    ).astype(jnp.bfloat16)
    grad_outgoing = grad_partial.reshape(row_count * col_count, owned_rows, in_width)
    grad_received = lax.all_to_all(
        grad_outgoing, ("row", "col"), split_axis=0, concat_axis=2, tiled=True
    )
    grad_summed = grad_received.reshape(owned_rows, row_count, col_count, in_width).astype(
        jnp.float32
    )
    dx_section = (
        jnp.sum(grad_summed, axis=2).reshape(owned_rows, row_count * in_width).astype(jnp.bfloat16)
    )
    return (y_next, dx_section)


def solution(mesh):
    return jax.shard_map(
        local,
        mesh=mesh,
        in_specs=(
            P("section", "row"),
            P(("section", "row"), "col"),
            P("section", "row", "col", None, None, None),
            P("section", "row", "col", None),
            P("section", "row", "col", None),
            P("section", "row", "col"),
            P("section", None),
            P("section", None),
        ),
        out_specs=(P(("section", "row", "col"), None), P(("section", "row", "col"), None)),
        check_vma=False,
    )
```

profile of v0, /device:TPU:1, one launch (start us, length us, event | category | flops | bytes accessed | tf_op | source)
XLA Modules:
  0.0 134.3 jit_solution(12094650554060465217)
XLA Ops:
  7.2 0.0 copy-start
  7.2 0.0 all-gather.2.cloned.1.call-start
  7.2 1.3 fusion.28
  8.5 0.7 add_compare_fusion
  9.2 1.7 %broadcast_select_fusion = bf16[32,3072]{1,0:T(8,128)(2,1)} fusion(bf16[32,3072]{1,0:T(8,128)(2,1)} %param.9, pred[32]{0:T(512)(128)(4,1)S(1)} %add_compare_fusion), kind=kLoop, calls=%fused_computation.20 | loop fusion | flops 98304 | bytes 393248 | tf_op jit(solution)/shard_map/jit(_where)/select_n | solution.py:50
  10.9 0.0 all-gather.2.cloned.1.call-update
  11.6 0.7 multiply_bitcast_fusion
  12.2 0.1 iota_add_fusion
  12.3 0.1 add.97
  12.4 0.1 add.94
  12.5 0.7 fusion.25
  13.2 4.2 %bitcast_multiply_fusion = bf16[115,128,128]{2,1,0:T(8,128)(2,1)} fusion(bf16[1,1,1,115,128,128]{5,4,3,2,1,0:T(8,128)(2,1)} %param.10, bf16[115]{0:T(256)(128)(2,1)S(1)} %compare_convert_fusion), kind=kLoop, calls=%fused_computation.9 | loop fusion | flops 1884160 | bytes 7536870 | tf_op jit(solution)/shard_map/mul | solution.py:27
  17.4 6.0 %broadcast_in_dim.45 = bf16[12,24,128,128]{3,2,1,0:T(8,128)(2,1)} broadcast(bf16[]{:T(256)} %constant.9.clone.1), dimensions={} | broadcast | bytes 9437186 | tf_op jit(solution)/shard_map/broadcast_in_dim | solution.py:25
  23.4 27.1 %scatter_fusion = bf16[12,24,128,128]{3,2,1,0:T(8,128)(2,1)} fusion(bf16[12,24,128,128]{3,2,1,0:T(8,128)(2,1)} %broadcast_in_dim.45, s32[115]{0:T(128)S(1)} %fusion.25, bf16[115,128,128]{2,1,0:T(8,128)(2,1)} %bitcast_multiply_fusion), kind=kCustom, calls=%fused_computation.1 | custom fusion | flops 1884160 | bytes 11305880 | tf_op jit(solution)/shard_map/scatter-add | solution.py:26
  50.6 14.6 %copy.13 = bf16[12,128,24,128]{3,2,1,0:T(8,128)(2,1)} copy(bf16[12,128,24,128]{3,1,2,0:T(8,128)(2,1)} %bitcast.52) | data formatting | bytes 18874368 | tf_op jit(solution)/shard_map/transpose | solution.py:29
  65.2 0.0 copy-done
  65.2 1.3 gather_fusion
  66.5 0.6 broadcast_compare_fusion
  67.1 7.5 %fusion.9 = bf16[32,8,3072]{2,1,0:T(8,128)(2,1)} fusion(bf16[192,8,24,128]{3,2,1,0:T(8,128)(2,1)} %bitcast.53, bf16[256,1536]{1,0:T(8,128)(2,1)S(1)} %gather_fusion, pred[256]{0:T(512)(128)(4,1)S(1)} %get-tuple-element.3, pred[256]{0:T(512)(128)(4,1)S(1)} %get-tuple-element.2), kind=kOutput, calls=%fused_computation.10 | convolution fusion | flops 2417491968 | bytes 11796992 | tf_op jit(solution)/shard_map/dot_general | solution.py:40
  74.7 10.6 %all-to-all-start = ((bf16[32,8,3072]{2,1,0:T(8,128)(2,1)}), bf16[32,8,3072]{2,1,0:T(8,128)(2,1)S(1)}, u32[]{:S(2)}, u32[]{:S(2)}) async-start(bf16[32,8,3072]{2,1,0:T(8,128)(2,1)} %fusion.9), calls=%async_computation | async-start | bytes 3145728 | tf_op jit(solution)/shard_map/all_to_all | solution.py:44
  85.3 0.0 all-gather.2.cloned.1.call-done
  85.3 7.7 %fusion.15 = bf16[32,8,1536]{2,1,0:T(8,128)(2,1)} fusion(bf16[256,3072]{1,0:T(8,128)(2,1)} %all-gather.2.cloned.1.call-done, bf16[192,8,24,128]{3,2,1,0:T(8,128)(2,1)} %bitcast.54), kind=kOutput, calls=%fused_computation.12 | convolution fusion | flops 2416312320 | bytes 11796480 | tf_op jit(solution)/shard_map/dot_general | solution.py:51
  93.0 13.7 %all-to-all-done = bf16[32,8,3072]{2,1,0:T(8,128)(2,1)S(1)} async-done(((bf16[32,8,3072]{2,1,0:T(8,128)(2,1)}), bf16[32,8,3072]{2,1,0:T(8,128)(2,1)S(1)}, u32[]{:S(2)}, u32[]{:S(2)}) %all-to-all-start) | async-done | bytes 1572896 | tf_op jit(solution)/shard_map/all_to_all | solution.py:44
  106.7 5.6 %all-to-all-start.1 = ((bf16[32,8,1536]{2,1,0:T(8,128)(2,1)}), bf16[32,8,1536]{2,1,0:T(8,128)(2,1)S(1)}, u32[]{:S(2)}, u32[]{:S(2)}) async-start(bf16[32,8,1536]{2,1,0:T(8,128)(2,1)} %fusion.15), calls=%async_computation.1 | async-start | bytes 1572864 | tf_op jit(solution)/shard_map/all_to_all | solution.py:58
  112.3 2.0 %copy.14 = bf16[1,8,32,3072]{3,2,1,0:T(8,128)(2,1)} copy(bf16[1,8,32,3072]{3,1,2,0:T(8,128)(2,1)S(1)} %bitcast.55) | data formatting | bytes 3145728 | tf_op jit(solution)/shard_map/all_to_all | solution.py:44
  114.3 2.9 %reshape.169 = bf16[8,8,12288]{2,1,0:T(8,128)(2,1)S(1)} reshape(bf16[1,8,32,3072]{3,2,1,0:T(8,128)(2,1)} %copy.14) | data formatting | bytes 3145728 | tf_op jit(solution)/shard_map/reshape | solution.py:45
  117.2 1.0 reduce_sum.21
  118.3 1.5 %collective-permute-start = (bf16[8,12288]{1,0:T(8,128)(2,1)S(1)}, bf16[8,12288]{1,0:T(8,128)(2,1)S(1)}, u32[]{:S(2)}, u32[]{:S(2)}) collective-permute-start(bf16[8,12288]{1,0:T(8,128)(2,1)S(1)} %reduce_sum.21), channel_id=1, source_target_pairs={{0,32},{32,64},{64,96},{96,128},{128,160},{160,192},{192,224},{224... | collective-permute-start | bytes 589832 | tf_op jit(solution)/shard_map/ppermute | solution.py:10
  119.8 4.0 %collective-permute-done = bf16[8,12288]{1,0:T(8,128)(2,1)S(1)} collective-permute-done((bf16[8,12288]{1,0:T(8,128)(2,1)S(1)}, bf16[8,12288]{1,0:T(8,128)(2,1)S(1)}, u32[]{:S(2)}, u32[]{:S(2)}) %collective-permute-start) | collective-permute-done | bytes 196640 | tf_op jit(solution)/shard_map/ppermute | solution.py:10
  123.8 2.1 %all-to-all-done.1 = bf16[32,8,1536]{2,1,0:T(8,128)(2,1)S(1)} async-done(((bf16[32,8,1536]{2,1,0:T(8,128)(2,1)}), bf16[32,8,1536]{2,1,0:T(8,128)(2,1)S(1)}, u32[]{:S(2)}, u32[]{:S(2)}) %all-to-all-start.1) | async-done | bytes 786464 | tf_op jit(solution)/shard_map/all_to_all | solution.py:58
  126.0 0.8 bitcast_reduce_fusion
  126.7 0.7 copy.35
  (3 shorter events, 0.0 us)
Async XLA Ops:
  7.2 58.0 %copy-start = (bf16[256,1536]{1,0:T(8,128)(2,1)S(1)}, bf16[256,1536]{1,0:T(8,128)(2,1)}, u32[]{:S(2)}) copy-start(bf16[256,1536]{1,0:T(8,128)(2,1)} %param.8) | copy-start | bytes 2359300
  7.2 78.1 %all-gather.2.cloned.1.call-start = ((), (), s32[]{:S(2)}) async-start(), calls=%async_computation.2 | async-start | bytes 1769472 | tf_op jit(solution)/shard_map/all_gather | solution.py:52
  74.7 32.0 %all-to-all-start = ((bf16[32,8,3072]{2,1,0:T(8,128)(2,1)}), bf16[32,8,3072]{2,1,0:T(8,128)(2,1)S(1)}, u32[]{:S(2)}, u32[]{:S(2)}) async-start(bf16[32,8,3072]{2,1,0:T(8,128)(2,1)} %fusion.9), calls=%async_computation | async-start | bytes 3145728 | tf_op jit(solution)/shard_map/all_to_all | solution.py:44
  106.7 19.2 %all-to-all-start.1 = ((bf16[32,8,1536]{2,1,0:T(8,128)(2,1)}), bf16[32,8,1536]{2,1,0:T(8,128)(2,1)S(1)}, u32[]{:S(2)}, u32[]{:S(2)}) async-start(bf16[32,8,1536]{2,1,0:T(8,128)(2,1)} %fusion.15), calls=%async_computation.1 | async-start | bytes 1572864 | tf_op jit(solution)/shard_map/all_to_all | solution.py:58
  118.3 5.6 %collective-permute-start = (bf16[8,12288]{1,0:T(8,128)(2,1)S(1)}, bf16[8,12288]{1,0:T(8,128)(2,1)S(1)}, u32[]{:S(2)}, u32[]{:S(2)}) collective-permute-start(bf16[8,12288]{1,0:T(8,128)(2,1)S(1)} %reduce_sum.21), channel_id=1, source_target_pairs={{0,32},{32,64},{64,96},{96,128},{128,160},{160,192},{192,224},{224... | collective-permute-start | bytes 589832 | tf_op jit(solution)/shard_map/ppermute | solution.py:10
Sparse Core Ops, SparseCore 0:
  11.0 37.7 all-gather.1
where the time goes:
time: 135 us; the launch traced here: 134 us
  other arithmetic  37.6 us (28%)
  local copies, waits for them, and re-layouts  29.1 us (22%)
  waiting for transfers between devices  19.9 us (15%)
  starting transfers between devices  17.7 us (13%)
  matrix products  15.2 us (11%)
  between operations  14.8 us (11%)
    scatter-add x1, other arithmetic, local(): dense_blocks.at[blk_row.reshape(slot_total), blk_col.reshape(slot_total)]  27.1 us
    transpose x1, local copies, waits for them, and re-layouts, local(): jnp.transpose(dense_blocks, (0, 2, 1, 3)).reshape(in_width, out_width)  14.6 us
    all_to_all x1, waiting for transfers between devices, local(): lax.all_to_all(outgoing, ('row', 'col'), split_axis=0, concat_axis=2, til...  13.7 us
    all_to_all x1, starting transfers between devices, local(): lax.all_to_all(outgoing, ('row', 'col'), split_axis=0, concat_axis=2, til...  10.6 us
    dot_general x1, matrix products, local(): lax.dot_general(lax.all_gather(grad_kept, 'row', axis=0, tiled=True), den...  7.69 us
    dot_general x1, matrix products, local(): jnp.dot(ordered_rows, dense_weight, preferred_element_type=jnp.float32)  7.55 us
    broadcast_in_dim x1, local copies, waits for them, and re-layouts, local(): jnp.zeros((block_rows, block_cols, block_size, block_size), weights.dtype)  6.03 us
    all_to_all x1, starting transfers between devices, local(): lax.all_to_all(grad_outgoing, ('row', 'col'), split_axis=0, concat_axis=2...  5.56 us
  transfers between devices with their start and end apart: 4, of which 3 were waited for; matrix products, arithmetic and copies ran while one was open for 57% of the time, Pallas kernels for 0%

commit v1 on v0

v1 whole, which is shorter than its diff:
```python
import functools

import jax
import jax.numpy as jnp
from jax import lax
from jax.experimental import pallas as pl
from jax.experimental.pallas import tpu as pltpu
from jax.sharding import PartitionSpec as P

MESH = pl.DeviceIdType.MESH
F32 = jnp.float32
BF16 = jnp.bfloat16
FWD_UNITS = 4
BWD_UNITS = 2


def kernel(
    sizes,
    slot_ref,
    tok_ref,
    owner_ref,
    x_hbm,
    dy_hbm,
    w_hbm,
    y_out,
    dx_out,
    w,
    x,
    xp,
    dy_all,
    part,
    pair_in,
    summed,
    fwd_relay,
    fwd_direct,
    fwd_comb,
    fwd_fin,
    bpart,
    bwd_relay,
    bwd_direct,
    bwd_comb,
    bwd_fin,
    load_sem,
    gather_send,
    gather_recv,
    pair_send,
    pair_recv,
    fring_send,
    fring_recv,
    ffin_send,
    y_recv,
    bring_send,
    bring_recv,
    bfin_send,
    dx_recv,
):
    sections, rows, cols, block_rows, block_cols = sizes
    blk = w.shape[1]
    slot_total = w_hbm.shape[0]
    tokens, in_width = x.shape
    out_width = dy_all.shape[2]
    shard = dy_all.shape[1]
    fwd_width = out_width // FWD_UNITS
    bwd_width = in_width // BWD_UNITS

    sec = lax.axis_index("section")
    row = lax.axis_index("row")
    col = lax.axis_index("col")
    height, core = row // 2, row % 2
    ring = rows // 2
    later_sec = lax.rem(sec + 1, sections)
    earlier_sec = lax.rem(sec + sections - 1, sections)

    def high(by):
        return lax.rem(height + by + ring, ring)

    def across(by):
        return lax.rem(col + by + cols, cols)

    sibling = (sec, height * 2 + 1 - core, col)

    def tall(by):
        return (sec, high(by) * 2 + core, col)

    def wide(by):
        return (sec, row, across(by))

    load_w = pltpu.make_async_copy(w_hbm, w.at[pl.ds(0, slot_total)], load_sem.at[0])
    load_x = pltpu.make_async_copy(x_hbm, x, load_sem.at[1])
    load_dy = pltpu.make_async_copy(dy_hbm, dy_all.at[row], load_sem.at[2])
    load_dy.start()
    load_x.start()
    load_w.start()

    barrier = pltpu.get_barrier_semaphore()

    def greet(device):
        pl.semaphore_signal(barrier, inc=1, device_id=device, device_id_type=MESH)

    for by in range(1, rows):
        greet((sec, lax.rem(row + by, rows), col))
    greet(wide(1))
    greet(wide(-1))
    for c in range(cols):
        greet((later_sec, row, c))
        greet((earlier_sec, row, c))
    w[slot_total] = jnp.zeros((blk, blk), BF16)
    pl.semaphore_wait(barrier, rows + 1 + 2 * cols)

    def gather(k, src_row, lo, width, device):
        place = dy_all.at[src_row, :, pl.ds(lo, width)]
        return pltpu.make_async_remote_copy(
            src_ref=place,
            dst_ref=place,
            send_sem=gather_send.at[k],
            recv_sem=gather_recv.at[k],
            device_id=device,
            device_id_type=MESH,
        )

    half = out_width // 2
    below, above, far = high(-1) * 2 + core, high(1) * 2 + core, high(2) * 2 + core
    twin = 1 - 2 * core

    load_dy.wait()
    g_up = gather(0, row, 0, out_width, tall(1))
    g_down = gather(1, row, 0, out_width, tall(-1))
    g_own = gather(2, row, 0, out_width, sibling)
    g_up.start()
    g_down.start()
    g_own.start()

    limit = tok_ref[0, 0]
    blocks = owner_ref.shape[1]
    length = tokens // blocks
    half_rows = tokens // 2

    def delivered(m):
        k = m // half_rows
        rest = m % half_rows
        return ((rest // shard) * 2 + k) * shard + rest % shard

    place = delivered(lax.broadcasted_iota(jnp.int32, (blocks, tokens), 1)) // length
    spread = (place == lax.broadcasted_iota(jnp.int32, (blocks, tokens), 0)).astype(F32).astype(BF16)
    owners = jnp.broadcast_to(owner_ref[...].astype(F32), (8, blocks)).astype(BF16)
    owner_row = jnp.dot(owners, spread, preferred_element_type=F32)[0:1]
    inner = (lax.broadcasted_iota(jnp.int32, (1, tokens), 1) % length).astype(F32)
    source = owner_row * length + inner
    source = jnp.where(source < limit.astype(F32), source, -1.0)
    token = lax.broadcasted_iota(jnp.int32, (tokens, tokens), 0).astype(F32)
    pick = jnp.where(token == source, 1.0, 0.0).astype(F32).T.astype(BF16)
    load_x.wait()
    xp[...] = jnp.dot(pick, x[...], preferred_element_type=F32).astype(BF16)
    load_w.wait()

    def fwd_dot(u):
        def tile(n, carry):
            first = (u * (fwd_width // (2 * blk)) + n) * 2
            rhs = jnp.concatenate(
                [
                    jnp.concatenate(
                        [w[slot_ref[r * block_cols + first + j]] for j in range(2)], axis=1
                    )
                    for r in range(block_rows)
                ],
                axis=0,
            )
            out = jnp.dot(xp[...], rhs, preferred_element_type=F32)
            at = pl.ds(pl.multiple_of(n * 2 * blk, 2 * blk), 2 * blk)
            part[u, :, :, at] = out.astype(BF16).reshape(2, half_rows, 2 * blk)
            return carry

        lax.fori_loop(0, fwd_width // (2 * blk), tile, 0)

    def pair_copy(u):
        return pltpu.make_async_remote_copy(
            src_ref=part.at[u, 1 - core],
            dst_ref=pair_in.at[u],
            send_sem=pair_send.at[u],
            recv_sem=pair_recv.at[u],
            device_id=sibling,
            device_id_type=MESH,
        )

    def fwd_ring(u, k):
        way = 1 if u % 2 == 0 else -1
        by, dst, to = ((2, fwd_relay, way), (-way, fwd_direct, -way), (way, fwd_comb, way))[k]
        return pltpu.make_async_remote_copy(
            src_ref=summed.at[u, high(by)],
            dst_ref=dst.at[u],
            send_sem=fring_send.at[u, k],
            recv_sem=fring_recv.at[u, k],
            device_id=tall(to),
            device_id_type=MESH,
        )

    def fwd_pair(u):
        pair_copy(u).wait_recv()
        both = part[u, core].astype(F32) + pair_in[u].astype(F32)
        summed[u] = both.astype(BF16).reshape(ring, shard, fwd_width)
        fwd_ring(u, 0).start()
        fwd_ring(u, 1).start()

    def fwd_mid(u):
        way = 1 if u % 2 == 0 else -1
        fwd_ring(u, 0).wait_recv()
        there = high(way)
        summed[u, there] = (summed[u, there].astype(F32) + fwd_relay[u].astype(F32)).astype(BF16)
        fwd_ring(u, 2).start()

    def y_copy(u, c):
        return pltpu.make_async_remote_copy(
            src_ref=fwd_fin.at[u, c],
            dst_ref=y_out.at[:, pl.ds(pl.multiple_of(col * out_width + u * fwd_width, 128), fwd_width)],
            send_sem=ffin_send.at[u, c],
            recv_sem=y_recv,
            device_id=(later_sec, row, c),
            device_id_type=MESH,
        )

    def fwd_end(u):
        fwd_ring(u, 1).wait_recv()
        fwd_ring(u, 2).wait_recv()
        total = summed[u, height].astype(F32) + fwd_direct[u].astype(F32) + fwd_comb[u].astype(F32)
        fwd_fin[u] = total.reshape(cols, shard // cols, fwd_width).astype(BF16)
        for c in range(cols):
            y_copy(u, c).start()

    def bwd_dot(v):
        def tile(n, carry):
            first = (v * (bwd_width // (2 * blk)) + n) * 2
            rhs = jnp.concatenate(
                [
                    jnp.concatenate(
                        [w[slot_ref[(first + j) * block_cols + c]] for j in range(2)], axis=0
                    )
                    for c in range(block_cols)
                ],
                axis=1,
            )
            out = lax.dot_general(
                dy_all[...].reshape(tokens, out_width),
                rhs,
                (((1,), (1,)), ((), ())),
                preferred_element_type=F32,
            )
            at = pl.ds(pl.multiple_of(n * 2 * blk, 2 * blk), 2 * blk)
            bpart[v, :, :, :, at] = out.reshape(rows, cols, shard // cols, 2 * blk).astype(BF16)
            return carry

        lax.fori_loop(0, bwd_width // (2 * blk), tile, 0)

    def bwd_ring(v, k):
        way = 1 if v % 2 == 0 else -1
        by, dst, to = ((2, bwd_relay, way), (-way, bwd_direct, -way), (way, bwd_comb, way))[k]
        return pltpu.make_async_remote_copy(
            src_ref=bpart.at[v, :, across(by)],
            dst_ref=dst.at[v],
            send_sem=bring_send.at[v, k],
            recv_sem=bring_recv.at[v, k],
            device_id=wide(to),
            device_id_type=MESH,
        )

    def bwd_mid(v):
        way = 1 if v % 2 == 0 else -1
        bwd_ring(v, 0).wait_recv()
        there = across(way)
        bpart[v, :, there] = (bpart[v, :, there].astype(F32) + bwd_relay[v].astype(F32)).astype(BF16)
        bwd_ring(v, 2).start()

    def dx_at(v):
        return dx_out.at[:, pl.ds(pl.multiple_of(row * in_width + v * bwd_width, 128), bwd_width)]

    def dx_copy(v, by):
        to = lax.rem(row + by, rows)
        return pltpu.make_async_remote_copy(
            src_ref=bwd_fin.at[v, to],
            dst_ref=dx_at(v),
            send_sem=bfin_send.at[v, by],
            recv_sem=dx_recv,
            device_id=(sec, to, col),
            device_id_type=MESH,
        )

    def dx_own(v):
        return pltpu.make_async_copy(bwd_fin.at[v, row], dx_at(v), bfin_send.at[v, 0])

    def bwd_end(v):
        bwd_ring(v, 1).wait_recv()
        bwd_ring(v, 2).wait_recv()
        total = bpart[v, :, col].astype(F32) + bwd_direct[v].astype(F32) + bwd_comb[v].astype(F32)
        bwd_fin[v] = total.astype(BF16)
        for by in range(1, rows):
            dx_copy(v, by).start()
        dx_own(v).start()

    fwd_dot(0)
    pair_copy(0).start()
    fwd_dot(1)
    pair_copy(1).start()
    fwd_pair(0)

    gather(0, below, 0, out_width, tall(1)).wait_recv()
    g_on_up = gather(3, below, 0, half, tall(1))
    g_on_up.start()
    g_below = gather(5, below, 0, out_width, sibling)
    g_below.start()
    gather(1, above, 0, out_width, tall(-1)).wait_recv()
    g_on_down = gather(4, above, half, half, tall(-1))
    g_on_down.start()
    g_above = gather(6, above, 0, out_width, sibling)
    g_above.start()

    fwd_dot(2)
    pair_copy(2).start()
    fwd_pair(1)
    fwd_dot(3)
    pair_copy(3).start()
    fwd_pair(2)
    gather(3, far, 0, half, tall(1)).wait_recv()
    g_far_low = gather(7, far, 0, half, sibling)
    g_far_low.start()
    gather(4, far, half, half, tall(-1)).wait_recv()
    g_far_high = gather(8, far, half, half, sibling)
    g_far_high.start()
    fwd_pair(3)
    fwd_mid(0)
    fwd_mid(1)

    gather(2, row + twin, 0, out_width, sibling).wait_recv()
    gather(5, below + twin, 0, out_width, sibling).wait_recv()
    gather(6, above + twin, 0, out_width, sibling).wait_recv()
    gather(7, far + twin, 0, half, sibling).wait_recv()
    gather(8, far + twin, half, half, sibling).wait_recv()

    bwd_dot(0)
    bwd_ring(0, 0).start()
    bwd_ring(0, 1).start()
    fwd_mid(2)
    fwd_mid(3)
    fwd_end(0)
    fwd_end(1)
    bwd_dot(1)
    bwd_ring(1, 0).start()
    bwd_ring(1, 1).start()
    bwd_mid(0)
    fwd_end(2)
    fwd_end(3)
    bwd_mid(1)
    bwd_end(0)
    bwd_end(1)

    for copy in (g_up, g_down, g_own, g_on_up, g_on_down, g_below, g_above, g_far_low, g_far_high):
        copy.wait_send()
    for u in range(FWD_UNITS):
        pair_copy(u).wait_send()
        for k in range(3):
            fwd_ring(u, k).wait_send()
        for c in range(cols):
            y_copy(u, c).wait_send()
    for v in range(BWD_UNITS):
        for k in range(3):
            bwd_ring(v, k).wait_send()
        for by in range(1, rows):
            dx_copy(v, by).wait_send()
        dx_own(v).wait()

    pltpu.make_async_remote_copy(
        src_ref=y_out,
        dst_ref=y_out,
        send_sem=y_recv,
        recv_sem=y_recv,
        device_id=sibling,
        device_id_type=MESH,
    ).wait_recv()
    others = dx_out.at[:, pl.ds(0, (rows - 1) * in_width)]
    pltpu.make_async_remote_copy(
        src_ref=others,
        dst_ref=others,
        send_sem=dx_recv,
        recv_sem=dx_recv,
        device_id=sibling,
        device_id_type=MESH,
    ).wait_recv()


def local(x_fwd, dy_bwd, w_blocks, blk_row, blk_col, blk_count, tok_count, owner_order):
    sections = lax.axis_size("section")
    rows = lax.axis_size("row")
    cols = lax.axis_size("col")
    ring = rows // 2
    tokens, in_width = x_fwd.shape
    shard, out_width = dy_bwd.shape
    slot_total = w_blocks.shape[3]
    blk = w_blocks.shape[5]
    block_rows, block_cols = in_width // blk, out_width // blk
    positions = block_rows * block_cols
    owned = tokens // (rows * cols)
    fwd_width = out_width // FWD_UNITS
    bwd_width = in_width // BWD_UNITS

    slots = jnp.arange(slot_total)
    where_to = blk_row.reshape(slot_total) * block_cols + blk_col.reshape(slot_total)
    where_to = jnp.where(slots < blk_count.reshape(()), where_to, -1)
    slot_of = jnp.min(
        jnp.where(where_to[None, :] == jnp.arange(positions)[:, None], slots[None, :], slot_total), axis=1
    ).astype(jnp.int32)

    dma = pltpu.SemaphoreType.DMA
    y_raw, dx_raw = pl.pallas_call(
        functools.partial(kernel, (sections, rows, cols, block_rows, block_cols)),
        out_shape=(
            jax.ShapeDtypeStruct((owned, cols * out_width), BF16),
            jax.ShapeDtypeStruct((owned, rows * in_width), BF16),
        ),
        in_specs=[
            pl.BlockSpec(memory_space=pltpu.SMEM),
            pl.BlockSpec(memory_space=pltpu.SMEM),
            pl.BlockSpec(memory_space=pltpu.VMEM),
            pl.BlockSpec(memory_space=pl.ANY),
            pl.BlockSpec(memory_space=pl.ANY),
            pl.BlockSpec(memory_space=pl.ANY),
        ],
        out_specs=(pl.BlockSpec(memory_space=pl.ANY), pl.BlockSpec(memory_space=pl.ANY)),
        scratch_shapes=[
            pltpu.VMEM((slot_total + 1, blk, blk), BF16),
            pltpu.VMEM((tokens, in_width), BF16),
            pltpu.VMEM((tokens, in_width), BF16),
            pltpu.VMEM((rows, shard, out_width), BF16),
            pltpu.VMEM((FWD_UNITS, 2, tokens // 2, fwd_width), BF16),
            pltpu.VMEM((FWD_UNITS, tokens // 2, fwd_width), BF16),
            pltpu.VMEM((FWD_UNITS, ring, shard, fwd_width), BF16),
            pltpu.VMEM((FWD_UNITS, shard, fwd_width), BF16),
            pltpu.VMEM((FWD_UNITS, shard, fwd_width), BF16),
            pltpu.VMEM((FWD_UNITS, shard, fwd_width), BF16),
            pltpu.VMEM((FWD_UNITS, cols, owned, fwd_width), BF16),
            pltpu.VMEM((BWD_UNITS, rows, cols, owned, bwd_width), BF16),
            pltpu.VMEM((BWD_UNITS, rows, owned, bwd_width), BF16),
            pltpu.VMEM((BWD_UNITS, rows, owned, bwd_width), BF16),
            pltpu.VMEM((BWD_UNITS, rows, owned, bwd_width), BF16),
            pltpu.VMEM((BWD_UNITS, rows, owned, bwd_width), BF16),
            dma((3,)),
            dma((9,)),
            dma((9,)),
            dma((FWD_UNITS,)),
            dma((FWD_UNITS,)),
            dma((FWD_UNITS, 3)),
            dma((FWD_UNITS, 3)),
            dma((FWD_UNITS, cols)),
            dma,
            dma((BWD_UNITS, 3)),
            dma((BWD_UNITS, 3)),
            dma((BWD_UNITS, rows)),
            dma,
        ],
        compiler_params=pltpu.CompilerParams(
            collective_id=0, has_side_effects=True, vmem_limit_bytes=40 * 1024 * 1024
        ),
    )(
        slot_of,
        tok_count,
        owner_order,
        x_fwd,
        dy_bwd,
        w_blocks.reshape(slot_total, blk, blk),
    )
    y_next = jnp.where(lax.axis_index("section") == 0, jnp.zeros_like(y_raw), y_raw)
    owner = (lax.axis_index("row") * cols + lax.axis_index("col")) * owned
    token = owner + lax.broadcasted_iota(jnp.int32, dx_raw.shape, 0)
    dx_section = jnp.where(token < tok_count[0, 1], dx_raw, jnp.zeros_like(dx_raw))
    return (y_next, dx_section)


def solution(mesh):
    return jax.shard_map(
        local,
        mesh=mesh,
        in_specs=(
            P("section", "row"),
            P(("section", "row"), "col"),
            P("section", "row", "col", None, None, None),
            P("section", "row", "col", None),
            P("section", "row", "col", None),
            P("section", "row", "col"),
            P("section", None),
            P("section", None),
        ),
        out_specs=(P(("section", "row", "col"), None), P(("section", "row", "col"), None)),
        check_vma=False,
    )
```

time: 135 us -> 56.1 us (0.42)
  Pallas kernels: 0 us -> 45.6 us
  other arithmetic: 37.6 us -> 2.25 us
  local copies, waits for them, and re-layouts: 29.1 us -> 6.67 us
  waiting for transfers between devices: 19.9 us -> 0 us
  starting transfers between devices: 17.7 us -> 0 us
  matrix products: 15.2 us -> 0 us
  between operations: 14.8 us -> 1.31 us
    pallas_call x0 -> x1, Pallas kernels: none -> 45.6 us  [local(): pl.pallas_call(functools.partial(kernel, (sections, rows, cols, block_row...]
    scatter-add x1 -> x0, other arithmetic: 27.1 us -> none  [local(): dense_blocks.at[blk_row.reshape(slot_total), blk_col.reshape(slot_total)]]
    all_to_all x2 -> x0, starting transfers between devices: 16.2 us -> none  [the longest x1 10.6 us: local(): lax.all_to_all(outgoing, ('row', 'col'), split_axis=0, concat_axis=2, til...]
    all_to_all x2 -> x0, waiting for transfers between devices: 15.8 us -> none  [the longest x1 13.7 us: local(): lax.all_to_all(outgoing, ('row', 'col'), split_axis=0, concat_axis=2, til...]
    dot_general x2 -> x0, matrix products: 15.2 us -> none  [the longest x1 7.69 us: local(): lax.dot_general(lax.all_gather(grad_kept, 'row', axis=0, tiled=True), den...]
    transpose x1 -> x0, local copies, waits for them, and re-layouts: 14.6 us -> none  [local(): jnp.transpose(dense_blocks, (0, 2, 1, 3)).reshape(in_width, out_width)]
    broadcast_in_dim x1 -> x0, local copies, waits for them, and re-layouts: 6.03 us -> none  [local(): jnp.zeros((block_rows, block_cols, block_size, block_size), weights.dtype)]
    mul x2 -> x0, other arithmetic: 4.86 us -> none  [the longest x1 4.2 us: local(): weights * live[:, None, None]]
  transfers between devices with their start and end apart: 4 -> 0, of which waited for: 3 -> 0; matrix products, arithmetic and copies ran while one was open for 57% -> 0% of each run, Pallas kernels for 0% -> 0%
where the time goes in v1:
time: 56.1 us; the launch traced here: 55.8 us
  Pallas kernels  45.6 us (81%)
  local copies, waits for them, and re-layouts  6.67 us (12%)
  other arithmetic  2.25 us (4%)
  between operations  1.31 us (2%)
    pallas_call x1, Pallas kernels, local(): pl.pallas_call(functools.partial(kernel, (sections, rows, cols, block_row...  45.6 us
    unnamed x10, local copies, waits for them, and re-layouts  5.43 us
    slice x1, local copies, waits for them, and re-layouts, local(): tok_count[0, 1]  1.24 us

profile of v1, /device:TPU:1, one launch (start us, length us, event | category | flops | bytes accessed | tf_op | source)
XLA Modules:
  0.0 55.8 jit_solution(11902492005868488278)
XLA Ops:
  1.3 1.2 %slice.3 = s32[1,1]{1,0:T(1,128)} slice(s32[1,2]{1,0:T(1,128)} %tok_ref.1), slice={[0:1], [1:2]} | slice | bytes 8 | tf_op jit(solution)/shard_map/slice | solution.py:471
  2.5 0.7 %add_compare_fusion = pred[8]{0:T(512)(128)(4,1)S(1)} fusion(s32[]{:T(128)} %bitcast.3, s32[]{:T(128)S(6)} %mul.20), kind=kLoop, calls=%fused_computation.5 | loop fusion | flops 16 | bytes 16 | tf_op jit(solution)/shard_map/lt | solution.py:471
  3.2 0.7 %compare_select_fusion = s32[115]{0:T(128)S(1)} fusion(s32[1,1,1,115]{3,2,1,0:T(1,128)} %param.12, s32[1,1,1,115]{3,2,1,0:T(1,128)} %param.11, s32[]{:T(128)} %bitcast.5), kind=kLoop, calls=%fused_computation.4 | loop fusion | flops 460 | bytes 1384 | tf_op jit(solution)/shard_map/jit(_where)/select_n | solution.py:405
  3.9 0.1 select_reduce_fusion.slot_ref
  4.0 0.0 copy-start
  4.0 2.1 %copy-done = bf16[1,1,1,115,128,128]{5,4,3,2,1,0:T(8,128)(2,1)S(1)} copy-done((bf16[1,1,1,115,128,128]{5,4,3,2,1,0:T(8,128)(2,1)S(1)}, bf16[1,1,1,115,128,128]{5,4,3,2,1,0:T(8,128)(2,1)}, u32[]{:S(2)}) %copy-start) | copy-done | bytes 3768344
  6.1 0.0 copy-start.1
  6.1 1.1 %copy-done.1 = bf16[256,1536]{1,0:T(8,128)(2,1)S(1)} copy-done((bf16[256,1536]{1,0:T(8,128)(2,1)S(1)}, bf16[256,1536]{1,0:T(8,128)(2,1)}, u32[]{:S(2)}) %copy-start.1) | copy-done | bytes 786456
  7.2 0.0 copy-start.2
  7.2 0.9 %copy-done.2 = bf16[32,3072]{1,0:T(8,128)(2,1)S(1)} copy-done((bf16[32,3072]{1,0:T(8,128)(2,1)S(1)}, bf16[32,3072]{1,0:T(8,128)(2,1)}, u32[]{:S(2)}) %copy-start.2) | copy-done | bytes 196632
  8.1 0.0 copy-start.3
  8.1 0.7 %copy-done.3 = s32[1,2]{1,0:T(1,128)S(1)} copy-done((s32[1,2]{1,0:T(1,128)S(1)}, s32[1,2]{1,0:T(1,128)}, u32[]{:S(2)}) %copy-start.3) | copy-done | bytes 32
  8.8 0.0 copy-start.4
  8.8 0.7 %copy-done.4 = s32[1,64]{1,0:T(1,128)S(1)} copy-done((s32[1,64]{1,0:T(1,128)S(1)}, s32[1,64]{1,0:T(1,128)}, u32[]{:S(2)}) %copy-start.4) | copy-done | bytes 280
  9.5 45.6 %shard_map.95 = (bf16[8,12288]{1,0:T(8,128)(2,1)S(1)}, bf16[8,12288]{1,0:T(8,128)(2,1)S(1)}) custom-call(s32[288]{0:T(512)S(1)} %select_reduce_fusion.slot_ref, s32[1,2]{1,0:T(1,128)S(1)} %copy-done.3, s32[1,64]{1,0:T(1,128)S(1)} %copy-done.4, bf16[256,1536]{1,0:T(8,128)(2,1)S(1)} %copy-done.1, bf16[32,3072]{1,0:T(8,128)(2,1)S(1)} %copy-done.2, ...), custom_call_target="tpu_custom_call" | custom-call | tf_op jit(solution)/shard_map/pallas_call | solution.py:411
  55.0 0.8 %broadcast_select_fusion = (bf16[8,12288]{1,0:T(8,128)(2,1)}, bf16[8,12288]{1,0:T(8,128)(2,1)}) fusion(bf16[8,12288]{1,0:T(8,128)(2,1)S(1)} %get-tuple-element.5, pred[8]{0:T(512)(128)(4,1)S(1)} %add_compare_fusion, bf16[8,12288]{1,0:T(8,128)(2,1)S(1)} %get-tuple-element.4, pred[]{:T(512)S(6)} %eq.16), kind=kLoop, calls=%fused_computation | loop fusion | flops 196608 | bytes 786441 | tf_op jit(solution)/shard_map/jit(_where)/select_n | solution.py:471
Async XLA Ops:
  4.0 2.1 %copy-start = (bf16[1,1,1,115,128,128]{5,4,3,2,1,0:T(8,128)(2,1)S(1)}, bf16[1,1,1,115,128,128]{5,4,3,2,1,0:T(8,128)(2,1)}, u32[]{:S(2)}) copy-start(bf16[1,1,1,115,128,128]{5,4,3,2,1,0:T(8,128)(2,1)} %param.10) | copy-start | bytes 11304964
  6.1 1.1 %copy-start.1 = (bf16[256,1536]{1,0:T(8,128)(2,1)S(1)}, bf16[256,1536]{1,0:T(8,128)(2,1)}, u32[]{:S(2)}) copy-start(bf16[256,1536]{1,0:T(8,128)(2,1)} %x_hbm.1) | copy-start | bytes 2359300
  7.2 0.9 %copy-start.2 = (bf16[32,3072]{1,0:T(8,128)(2,1)S(1)}, bf16[32,3072]{1,0:T(8,128)(2,1)}, u32[]{:S(2)}) copy-start(bf16[32,3072]{1,0:T(8,128)(2,1)} %dy_hbm.1) | copy-start | bytes 589828
  8.1 0.7 %copy-start.3 = (s32[1,2]{1,0:T(1,128)S(1)}, s32[1,2]{1,0:T(1,128)}, u32[]{:S(2)}) copy-start(s32[1,2]{1,0:T(1,128)} %tok_ref.1) | copy-start | bytes 28
  8.8 0.7 %copy-start.4 = (s32[1,64]{1,0:T(1,128)S(1)}, s32[1,64]{1,0:T(1,128)}, u32[]{:S(2)}) copy-start(s32[1,64]{1,0:T(1,128)} %owner_ref.1) | copy-start | bytes 772

commit v2 on v1

--- a/solution.py
+++ b/solution.py
@@ -10,20 +10,29 @@
 MESH = pl.DeviceIdType.MESH
 F32 = jnp.float32
 BF16 = jnp.bfloat16
-FWD_UNITS = 4
-BWD_UNITS = 2
+FWD_UNITS = 6
+BWD_UNITS = 6
+BWD_GROUP = 2
 
 
 def kernel(
     sizes,
-    slot_ref,
-    tok_ref,
-    owner_ref,
+    count_ref,
+    tok_hbm,
+    owner_hbm,
+    blk_row_hbm,
+    blk_col_hbm,
     x_hbm,
     dy_hbm,
     w_hbm,
     y_out,
     dx_out,
+    tok_ref,
+    owner_ref,
+    blk_row_ref,
+    blk_col_ref,
+    slot_ref,
+    slot_row,
     w,
     x,
     xp,
@@ -68,8 +77,6 @@
     col = lax.axis_index("col")
     height, core = row // 2, row % 2
     ring = rows // 2
-    later_sec = lax.rem(sec + 1, sections)
-    earlier_sec = lax.rem(sec + sections - 1, sections)
 
     def high(by):
         return lax.rem(height + by + ring, ring)
@@ -89,6 +96,19 @@
     load_x = pltpu.make_async_copy(x_hbm, x, load_sem.at[1])
     load_dy = pltpu.make_async_copy(dy_hbm, dy_all.at[row], load_sem.at[2])
     load_dy.start()
+    small = [
+        pltpu.make_async_copy(there, here, load_sem.at[4 + k])
+        for k, (there, here) in enumerate(
+            (
+                (blk_row_hbm, blk_row_ref),
+                (blk_col_hbm, blk_col_ref),
+                (tok_hbm, tok_ref),
+                (owner_hbm, owner_ref),
+            )
+        )
+    ]
+    for copy in small:
+        copy.start()
     load_x.start()
     load_w.start()
 
@@ -101,11 +121,20 @@
         greet((sec, lax.rem(row + by, rows), col))
     greet(wide(1))
     greet(wide(-1))
-    for c in range(cols):
-        greet((later_sec, row, c))
-        greet((earlier_sec, row, c))
-    w[slot_total] = jnp.zeros((blk, blk), BF16)
-    pl.semaphore_wait(barrier, rows + 1 + 2 * cols)
+
+    @pl.when(sec > 0)
+    def _():
+        for c in range(cols):
+            greet((sec - 1, row, c))
+
+
+    @pl.when(sec < sections - 1)
+    def _():
+        pl.semaphore_wait(barrier, rows + 1 + cols)
+
+    @pl.when(sec == sections - 1)
+    def _():
+        pl.semaphore_wait(barrier, rows + 1)
 
     def gather(k, src_row, lo, width, device):
         place = dy_all.at[src_row, :, pl.ds(lo, width)]
@@ -123,13 +152,38 @@
     twin = 1 - 2 * core
 
     load_dy.wait()
-    g_up = gather(0, row, 0, out_width, tall(1))
-    g_down = gather(1, row, 0, out_width, tall(-1))
-    g_own = gather(2, row, 0, out_width, sibling)
-    g_up.start()
-    g_down.start()
-    g_own.start()
-
+    gathers = [
+        gather(0, row, 0, half, tall(1)),
+        gather(1, row, half, half, tall(-1)),
+        gather(2, row, half, half, tall(1)),
+        gather(3, row, 0, half, tall(-1)),
+        gather(4, row, 0, out_width, sibling),
+    ]
+    for copy in gathers:
+        copy.start()
+
+    def hand_on(*copies):
+        for copy in copies:
+            copy.start()
+            gathers.append(copy)
+
+    for copy in small:
+        copy.wait()
+    w[slot_total] = jnp.zeros((blk, blk), BF16)
+
+    slot = lax.broadcasted_iota(jnp.int32, (1, slot_total), 1)
+    target = blk_row_ref[...] * block_cols + blk_col_ref[...]
+    target = jnp.where(slot < count_ref[0, 0, 0], target, -1)
+    target = jnp.concatenate([target, jnp.full((1, blk - slot_total), -1, jnp.int32)], axis=1)
+    target = jnp.broadcast_to(target, (8, blk)).T[:, 0:1]
+    held = jnp.where(
+        target == lax.broadcasted_iota(jnp.int32, (blk, slot_row.shape[1]), 1),
+        lax.broadcasted_iota(jnp.int32, (blk, slot_row.shape[1]), 0),
+        slot_total,
+    )
+    slot_row[...] = jnp.min(held, axis=0, keepdims=True)
+    load_slots = pltpu.make_async_copy(slot_row, slot_ref, load_sem.at[3])
+    load_slots.start()
     limit = tok_ref[0, 0]
     blocks = owner_ref.shape[1]
     length = tokens // blocks
@@ -151,6 +205,7 @@
     pick = jnp.where(token == source, 1.0, 0.0).astype(F32).T.astype(BF16)
     load_x.wait()
     xp[...] = jnp.dot(pick, x[...], preferred_element_type=F32).astype(BF16)
+    load_slots.wait()
     load_w.wait()
 
     def fwd_dot(u):
@@ -159,7 +214,7 @@
             rhs = jnp.concatenate(
                 [
                     jnp.concatenate(
-                        [w[slot_ref[r * block_cols + first + j]] for j in range(2)], axis=1
+                        [w[slot_ref[0, r * block_cols + first + j]] for j in range(2)], axis=1
                     )
                     for r in range(block_rows)
                 ],
@@ -214,7 +269,7 @@
             dst_ref=y_out.at[:, pl.ds(pl.multiple_of(col * out_width + u * fwd_width, 128), fwd_width)],
             send_sem=ffin_send.at[u, c],
             recv_sem=y_recv,
-            device_id=(later_sec, row, c),
+            device_id=(sec + 1, row, c),
             device_id_type=MESH,
         )
 
@@ -223,8 +278,11 @@
         fwd_ring(u, 2).wait_recv()
         total = summed[u, height].astype(F32) + fwd_direct[u].astype(F32) + fwd_comb[u].astype(F32)
         fwd_fin[u] = total.reshape(cols, shard // cols, fwd_width).astype(BF16)
-        for c in range(cols):
-            y_copy(u, c).start()
+
+        @pl.when(sec < sections - 1)
+        def _():
+            for c in range(cols):
+                y_copy(u, c).start()
 
     def bwd_dot(v):
         def tile(n, carry):
@@ -232,7 +290,7 @@
             rhs = jnp.concatenate(
                 [
                     jnp.concatenate(
-                        [w[slot_ref[(first + j) * block_cols + c]] for j in range(2)], axis=0
+                        [w[slot_ref[0, (first + j) * block_cols + c]] for j in range(2)], axis=0
                     )
                     for c in range(block_cols)
                 ],
@@ -245,7 +303,9 @@
                 preferred_element_type=F32,
             )
             at = pl.ds(pl.multiple_of(n * 2 * blk, 2 * blk), 2 * blk)
-            bpart[v, :, :, :, at] = out.reshape(rows, cols, shard // cols, 2 * blk).astype(BF16)
+            out = out.reshape(rows, cols, shard // cols, 2 * blk).astype(BF16)
+            for c in range(cols):
+                bpart[v, c, :, :, at] = out[:, c]
             return carry
 
         lax.fori_loop(0, bwd_width // (2 * blk), tile, 0)
@@ -254,7 +314,7 @@
         way = 1 if v % 2 == 0 else -1
         by, dst, to = ((2, bwd_relay, way), (-way, bwd_direct, -way), (way, bwd_comb, way))[k]
         return pltpu.make_async_remote_copy(
-            src_ref=bpart.at[v, :, across(by)],
+            src_ref=bpart.at[v, across(by)],
             dst_ref=dst.at[v],
             send_sem=bring_send.at[v, k],
             recv_sem=bring_recv.at[v, k],
@@ -266,114 +326,144 @@
         way = 1 if v % 2 == 0 else -1
         bwd_ring(v, 0).wait_recv()
         there = across(way)
-        bpart[v, :, there] = (bpart[v, :, there].astype(F32) + bwd_relay[v].astype(F32)).astype(BF16)
+        bpart[v, there] = (bpart[v, there].astype(F32) + bwd_relay[v].astype(F32)).astype(BF16)
         bwd_ring(v, 2).start()
 
-    def dx_at(v):
-        return dx_out.at[:, pl.ds(pl.multiple_of(row * in_width + v * bwd_width, 128), bwd_width)]
-
-    def dx_copy(v, by):
+    group_width = BWD_GROUP * bwd_width
+
+    def dx_at(g):
+        return dx_out.at[:, pl.ds(pl.multiple_of(row * in_width + g * group_width, 128), group_width)]
+
+    def dx_copy(g, by):
         to = lax.rem(row + by, rows)
         return pltpu.make_async_remote_copy(
-            src_ref=bwd_fin.at[v, to],
-            dst_ref=dx_at(v),
-            send_sem=bfin_send.at[v, by],
+            src_ref=bwd_fin.at[g, to],
+            dst_ref=dx_at(g),
+            send_sem=bfin_send.at[g, by],
             recv_sem=dx_recv,
             device_id=(sec, to, col),
             device_id_type=MESH,
         )
 
-    def dx_own(v):
-        return pltpu.make_async_copy(bwd_fin.at[v, row], dx_at(v), bfin_send.at[v, 0])
+    def dx_own(g):
+        return pltpu.make_async_copy(bwd_fin.at[g, row], dx_at(g), bfin_send.at[g, 0])
 
     def bwd_end(v):
         bwd_ring(v, 1).wait_recv()
         bwd_ring(v, 2).wait_recv()
-        total = bpart[v, :, col].astype(F32) + bwd_direct[v].astype(F32) + bwd_comb[v].astype(F32)
-        bwd_fin[v] = total.astype(BF16)
-        for by in range(1, rows):
-            dx_copy(v, by).start()
-        dx_own(v).start()
-
-    fwd_dot(0)
-    pair_copy(0).start()
-    fwd_dot(1)
-    pair_copy(1).start()
+        total = bpart[v, col].astype(F32) + bwd_direct[v].astype(F32) + bwd_comb[v].astype(F32)
+        token = lax.broadcasted_iota(jnp.int32, total.shape, 0) * shard + col * (shard // cols)
+        token = token + lax.broadcasted_iota(jnp.int32, total.shape, 1)
+        total = jnp.where(token < tok_ref[0, 1], total, 0.0).astype(BF16)
+        g = v // BWD_GROUP
+        bwd_fin[g, :, :, pl.ds((v % BWD_GROUP) * bwd_width, bwd_width)] = total
+        if v % BWD_GROUP == BWD_GROUP - 1:
+            for by in range(1, rows):
+                dx_copy(g, by).start()
+            dx_own(g).start()
+
+    def fwd_first(u):
+        fwd_dot(u)
+        pair_copy(u).start()
+
+    def bwd_first(v):
+        bwd_dot(v)
+        bwd_ring(v, 0).start()
+        bwd_ring(v, 1).start()
+
+    fwd_first(0)
+    fwd_first(1)
+    fwd_first(2)
+    fwd_first(3)
+    gather(0, below, 0, half, tall(1)).wait_recv()
+    hand_on(gather(5, below, 0, half, tall(1)), gather(6, below, 0, half, sibling))
+    gather(1, above, half, half, tall(-1)).wait_recv()
+    hand_on(gather(7, above, half, half, tall(-1)), gather(8, above, half, half, sibling))
     fwd_pair(0)
-
-    gather(0, below, 0, out_width, tall(1)).wait_recv()
-    g_on_up = gather(3, below, 0, half, tall(1))
-    g_on_up.start()
-    g_below = gather(5, below, 0, out_width, sibling)
-    g_below.start()
-    gather(1, above, 0, out_width, tall(-1)).wait_recv()
-    g_on_down = gather(4, above, half, half, tall(-1))
-    g_on_down.start()
-    g_above = gather(6, above, 0, out_width, sibling)
-    g_above.start()
-
-    fwd_dot(2)
-    pair_copy(2).start()
     fwd_pair(1)
-    fwd_dot(3)
-    pair_copy(3).start()
+    fwd_first(4)
     fwd_pair(2)
-    gather(3, far, 0, half, tall(1)).wait_recv()
-    g_far_low = gather(7, far, 0, half, sibling)
-    g_far_low.start()
-    gather(4, far, half, half, tall(-1)).wait_recv()
-    g_far_high = gather(8, far, half, half, sibling)
-    g_far_high.start()
+    fwd_first(5)
+    gather(2, below, half, half, tall(1)).wait_recv()
+    hand_on(gather(9, below, half, half, sibling))
+    gather(3, above, 0, half, tall(-1)).wait_recv()
+    hand_on(gather(10, above, 0, half, sibling))
     fwd_pair(3)
+    fwd_pair(4)
+    fwd_pair(5)
+    gather(5, far, 0, half, tall(1)).wait_recv()
+    hand_on(gather(11, far, 0, half, sibling))
+    gather(7, far, half, half, tall(-1)).wait_recv()
+    hand_on(gather(12, far, half, half, sibling))
     fwd_mid(0)
     fwd_mid(1)
-
-    gather(2, row + twin, 0, out_width, sibling).wait_recv()
-    gather(5, below + twin, 0, out_width, sibling).wait_recv()
-    gather(6, above + twin, 0, out_width, sibling).wait_recv()
-    gather(7, far + twin, 0, half, sibling).wait_recv()
-    gather(8, far + twin, half, half, sibling).wait_recv()
-
-    bwd_dot(0)
-    bwd_ring(0, 0).start()
-    bwd_ring(0, 1).start()
+    gather(4, row + twin, 0, out_width, sibling).wait_recv()
+    gather(6, below + twin, 0, half, sibling).wait_recv()
+    gather(8, above + twin, half, half, sibling).wait_recv()
+    gather(9, below + twin, half, half, sibling).wait_recv()
+    gather(10, above + twin, 0, half, sibling).wait_recv()
+    gather(11, far + twin, 0, half, sibling).wait_recv()
+    gather(12, far + twin, half, half, sibling).wait_recv()
+    bwd_first(0)
     fwd_mid(2)
+    bwd_first(1)
     fwd_mid(3)
+    bwd_first(2)
+    fwd_mid(4)
+    bwd_first(3)
+    bwd_first(4)
+    fwd_mid(5)
+    bwd_first(5)
+    bwd_mid(0)
     fwd_end(0)
     fwd_end(1)
-    bwd_dot(1)
-    bwd_ring(1, 0).start()
-    bwd_ring(1, 1).start()
-    bwd_mid(0)
     fwd_end(2)
+    bwd_mid(1)
     fwd_end(3)
-    bwd_mid(1)
+    fwd_end(4)
+    bwd_mid(2)
+    bwd_mid(3)
+    fwd_end(5)
+    bwd_mid(4)
+    bwd_mid(5)
     bwd_end(0)
     bwd_end(1)
-
-    for copy in (g_up, g_down, g_own, g_on_up, g_on_down, g_below, g_above, g_far_low, g_far_high):
+    bwd_end(2)
+    bwd_end(3)
+    bwd_end(4)
+    bwd_end(5)
+
+    for copy in gathers:
         copy.wait_send()
     for u in range(FWD_UNITS):
         pair_copy(u).wait_send()
         for k in range(3):
             fwd_ring(u, k).wait_send()
-        for c in range(cols):
-            y_copy(u, c).wait_send()
     for v in range(BWD_UNITS):
         for k in range(3):
             bwd_ring(v, k).wait_send()
+    for g in range(BWD_UNITS // BWD_GROUP):
         for by in range(1, rows):
-            dx_copy(v, by).wait_send()
-        dx_own(v).wait()
-
-    pltpu.make_async_remote_copy(
-        src_ref=y_out,
-        dst_ref=y_out,
-        send_sem=y_recv,
-        recv_sem=y_recv,
-        device_id=sibling,
-        device_id_type=MESH,
-    ).wait_recv()
+            dx_copy(g, by).wait_send()
+        dx_own(g).wait()
+
+    @pl.when(sec < sections - 1)
+    def _():
+        for u in range(FWD_UNITS):
+            for c in range(cols):
+                y_copy(u, c).wait_send()
+
+    @pl.when(sec > 0)
+    def _():
+        pltpu.make_async_remote_copy(
+            src_ref=y_out,
+            dst_ref=y_out,
+            send_sem=y_recv,
+            recv_sem=y_recv,
+            device_id=sibling,
+            device_id_type=MESH,
+        ).wait_recv()
+
     others = dx_out.at[:, pl.ds(0, (rows - 1) * in_width)]
     pltpu.make_async_remote_copy(
         src_ref=others,
@@ -395,17 +485,10 @@
     slot_total = w_blocks.shape[3]
     blk = w_blocks.shape[5]
     block_rows, block_cols = in_width // blk, out_width // blk
-    positions = block_rows * block_cols
+    table = pl.cdiv(block_rows * block_cols, 128) * 128
     owned = tokens // (rows * cols)
     fwd_width = out_width // FWD_UNITS
     bwd_width = in_width // BWD_UNITS
-
-    slots = jnp.arange(slot_total)
-    where_to = blk_row.reshape(slot_total) * block_cols + blk_col.reshape(slot_total)
-    where_to = jnp.where(slots < blk_count.reshape(()), where_to, -1)
-    slot_of = jnp.min(
-        jnp.where(where_to[None, :] == jnp.arange(positions)[:, None], slots[None, :], slot_total), axis=1
-    ).astype(jnp.int32)
 
     dma = pltpu.SemaphoreType.DMA
     y_raw, dx_raw = pl.pallas_call(
@@ -414,16 +497,16 @@
             jax.ShapeDtypeStruct((owned, cols * out_width), BF16),
             jax.ShapeDtypeStruct((owned, rows * in_width), BF16),
         ),
-        in_specs=[
-            pl.BlockSpec(memory_space=pltpu.SMEM),
-            pl.BlockSpec(memory_space=pltpu.SMEM),
-            pl.BlockSpec(memory_space=pltpu.VMEM),
-            pl.BlockSpec(memory_space=pl.ANY),
-            pl.BlockSpec(memory_space=pl.ANY),
-            pl.BlockSpec(memory_space=pl.ANY),
-        ],
+        in_specs=[pl.BlockSpec(memory_space=pltpu.SMEM)]
+        + [pl.BlockSpec(memory_space=pltpu.MemorySpace.HBM)] * 7,
         out_specs=(pl.BlockSpec(memory_space=pl.ANY), pl.BlockSpec(memory_space=pl.ANY)),
         scratch_shapes=[
+            pltpu.SMEM(tok_count.shape, jnp.int32),
+            pltpu.VMEM(owner_order.shape, jnp.int32),
+            pltpu.VMEM((1, slot_total), jnp.int32),
+            pltpu.VMEM((1, slot_total), jnp.int32),
+            pltpu.SMEM((1, table), jnp.int32),
+            pltpu.VMEM((1, table), jnp.int32),
             pltpu.VMEM((slot_total + 1, blk, blk), BF16),
             pltpu.VMEM((tokens, in_width), BF16),
             pltpu.VMEM((tokens, in_width), BF16),
@@ -435,14 +518,14 @@
             pltpu.VMEM((FWD_UNITS, shard, fwd_width), BF16),
             pltpu.VMEM((FWD_UNITS, shard, fwd_width), BF16),
             pltpu.VMEM((FWD_UNITS, cols, owned, fwd_width), BF16),
-            pltpu.VMEM((BWD_UNITS, rows, cols, owned, bwd_width), BF16),
+            pltpu.VMEM((BWD_UNITS, cols, rows, owned, bwd_width), BF16),
             pltpu.VMEM((BWD_UNITS, rows, owned, bwd_width), BF16),
             pltpu.VMEM((BWD_UNITS, rows, owned, bwd_width), BF16),
             pltpu.VMEM((BWD_UNITS, rows, owned, bwd_width), BF16),
-            pltpu.VMEM((BWD_UNITS, rows, owned, bwd_width), BF16),
-            dma((3,)),
-            dma((9,)),
-            dma((9,)),
+            pltpu.VMEM((BWD_UNITS // BWD_GROUP, rows, owned, BWD_GROUP * bwd_width), BF16),
+            dma((8,)),
+            dma((13,)),
+            dma((13,)),
             dma((FWD_UNITS,)),
             dma((FWD_UNITS,)),
             dma((FWD_UNITS, 3)),
@@ -451,24 +534,30 @@
             dma,
             dma((BWD_UNITS, 3)),
             dma((BWD_UNITS, 3)),
-            dma((BWD_UNITS, rows)),
+            dma((BWD_UNITS // BWD_GROUP, rows)),
             dma,
         ],
         compiler_params=pltpu.CompilerParams(
-            collective_id=0, has_side_effects=True, vmem_limit_bytes=40 * 1024 * 1024
+            collective_id=0, has_side_effects=True, vmem_limit_bytes=32 * 1024 * 1024
         ),
     )(
-        slot_of,
-        tok_count,
-        owner_order,
-        x_fwd,
-        dy_bwd,
-        w_blocks.reshape(slot_total, blk, blk),
+        blk_count,
+        *[
+            pltpu.with_memory_space_constraint(operand, pltpu.MemorySpace.HBM)
+            for operand in (
+                tok_count,
+                owner_order,
+                blk_row.reshape(1, slot_total),
+                blk_col.reshape(1, slot_total),
+                x_fwd,
+                dy_bwd,
+                w_blocks.reshape(slot_total, blk, blk),
+            )
+        ],
     )
-    y_next = jnp.where(lax.axis_index("section") == 0, jnp.zeros_like(y_raw), y_raw)
-    owner = (lax.axis_index("row") * cols + lax.axis_index("col")) * owned
-    token = owner + lax.broadcasted_iota(jnp.int32, dx_raw.shape, 0)
-    dx_section = jnp.where(token < tok_count[0, 1], dx_raw, jnp.zeros_like(dx_raw))
+    section = lax.axis_index("section")
+    y_next = jnp.where(section > 0, y_raw, jnp.zeros_like(y_raw))
+    dx_section = jnp.where(section >= 0, dx_raw, jnp.zeros_like(dx_raw))
     return (y_next, dx_section)
 
 

time: 56.1 us -> 39.2 us (0.70)
  Pallas kernels: 45.6 us -> 36.9 us
  local copies, waits for them, and re-layouts: 6.67 us -> 0 us
  other arithmetic: 2.25 us -> 0.78 us
    pallas_call x1, Pallas kernels: 45.6 us -> 36.9 us  [local(): pl.pallas_call(functools.partial(kernel, (sections, rows, cols, block_row...]
    unnamed x10 -> x0, local copies, waits for them, and re-layouts: 5.43 us -> none
    slice x1 -> x0, local copies, waits for them, and re-layouts: 1.24 us -> none  [local(): tok_count[0, 1]]
    select_n x2 -> x1, other arithmetic: 1.45 us -> 0.78 us  [local(): dx_section = jnp.where(section >= 0, dx_raw, jnp.zeros_like(dx_raw))]
    lt x1 -> x0, other arithmetic: 0.65 us -> none  [local(): token < tok_count[0, 1]]
where the time goes in v2:
time: 39.2 us; the launch traced here: 38.9 us
  Pallas kernels  36.9 us (94%)
  between operations  1.29 us (3%)
  other arithmetic  0.78 us (2%)
    pallas_call x1, Pallas kernels, local(): pl.pallas_call(functools.partial(kernel, (sections, rows, cols, block_row...  36.9 us

profile of v2, /device:TPU:1, one launch (start us, length us, event | category | flops | bytes accessed | tf_op | source)
XLA Modules:
  0.0 38.9 jit_solution(12443387297640438036)
XLA Ops:
  1.3 36.9 %shard_map.95 = (bf16[8,12288]{1,0:T(8,128)(2,1)S(1)}, bf16[8,12288]{1,0:T(8,128)(2,1)S(1)}) custom-call(s32[1,1,1]{2,1,0:T(1,128)S(6)} %copy.10.count_ref, s32[1,2]{1,0:T(1,128)} %tok_hbm.1, s32[1,64]{1,0:T(1,128)} %owner_hbm.1, s32[1,115]{1,0:T(1,128)} %bitcast.4, s32[1,115]{1,0:T(1,128)} %bitcast.5, bf16[256,1536]{1,0:T(8,128)(2,1)} %x_hbm.1, ...), custom_call_target="tpu_custom_call" | custom-call | tf_op jit(solution)/shard_map/pallas_call | solution.py:494
  38.2 0.8 %broadcast_select_fusion = (bf16[8,12288]{1,0:T(8,128)(2,1)}, bf16[8,12288]{1,0:T(8,128)(2,1)}) fusion(bf16[8,12288]{1,0:T(8,128)(2,1)S(1)} %get-tuple-element.5, pred[]{:T(512)S(6)} %ge.3, bf16[8,12288]{1,0:T(8,128)(2,1)S(1)} %get-tuple-element.4, pred[]{:T(512)S(6)} %gt.3), kind=kLoop, calls=%fused_computation | loop fusion | flops 196608 | bytes 786434 | tf_op jit(solution)/shard_map/jit(_where)/select_n | solution.py:560

commit v3 on v2

--- a/solution.py
+++ b/solution.py
@@ -12,7 +12,8 @@
 BF16 = jnp.bfloat16
 FWD_UNITS = 6
 BWD_UNITS = 6
-BWD_GROUP = 2
+BWD_GROUP = 1
+BWD_DOT = 2
 
 
 def kernel(
@@ -197,12 +198,12 @@
     place = delivered(lax.broadcasted_iota(jnp.int32, (blocks, tokens), 1)) // length
     spread = (place == lax.broadcasted_iota(jnp.int32, (blocks, tokens), 0)).astype(F32).astype(BF16)
     owners = jnp.broadcast_to(owner_ref[...].astype(F32), (8, blocks)).astype(BF16)
-    owner_row = jnp.dot(owners, spread, preferred_element_type=F32)[0:1]
-    inner = (lax.broadcasted_iota(jnp.int32, (1, tokens), 1) % length).astype(F32)
+    owner_row = jnp.dot(owners, spread, preferred_element_type=F32)
+    inner = (lax.broadcasted_iota(jnp.int32, (8, tokens), 1) % length).astype(F32)
     source = owner_row * length + inner
-    source = jnp.where(source < limit.astype(F32), source, -1.0)
-    token = lax.broadcasted_iota(jnp.int32, (tokens, tokens), 0).astype(F32)
-    pick = jnp.where(token == source, 1.0, 0.0).astype(F32).T.astype(BF16)
+    source = jnp.where(source < limit.astype(F32), source, -1.0).T[:, 0:1]
+    token = lax.broadcasted_iota(jnp.int32, (tokens, tokens), 1).astype(F32)
+    pick = jnp.where(token == source, 1.0, 0.0).astype(F32).astype(BF16)
     load_x.wait()
     xp[...] = jnp.dot(pick, x[...], preferred_element_type=F32).astype(BF16)
     load_slots.wait()
@@ -225,7 +226,7 @@
             part[u, :, :, at] = out.astype(BF16).reshape(2, half_rows, 2 * blk)
             return carry
 
-        lax.fori_loop(0, fwd_width // (2 * blk), tile, 0)
+        lax.fori_loop(0, fwd_width // (2 * blk), tile, 0, unroll=True)
 
     def pair_copy(u):
         return pltpu.make_async_remote_copy(
@@ -284,31 +285,28 @@
             for c in range(cols):
                 y_copy(u, c).start()
 
-    def bwd_dot(v):
-        def tile(n, carry):
-            first = (v * (bwd_width // (2 * blk)) + n) * 2
-            rhs = jnp.concatenate(
-                [
-                    jnp.concatenate(
-                        [w[slot_ref[0, (first + j) * block_cols + c]] for j in range(2)], axis=0
-                    )
-                    for c in range(block_cols)
-                ],
-                axis=1,
-            )
-            out = lax.dot_general(
-                dy_all[...].reshape(tokens, out_width),
-                rhs,
-                (((1,), (1,)), ((), ())),
-                preferred_element_type=F32,
-            )
-            at = pl.ds(pl.multiple_of(n * 2 * blk, 2 * blk), 2 * blk)
-            out = out.reshape(rows, cols, shard // cols, 2 * blk).astype(BF16)
-            for c in range(cols):
-                bpart[v, c, :, :, at] = out[:, c]
-            return carry
-
-        lax.fori_loop(0, bwd_width // (2 * blk), tile, 0)
+    def bwd_dot(p):
+        for v in range(p * BWD_DOT, (p + 1) * BWD_DOT):
+            for n in range(bwd_width // (2 * blk)):
+                first = (v * (bwd_width // (2 * blk)) + n) * 2
+                rhs = jnp.concatenate(
+                    [
+                        jnp.concatenate(
+                            [w[slot_ref[0, (first + j) * block_cols + c]] for j in range(2)], axis=0
+                        )
+                        for c in range(block_cols)
+                    ],
+                    axis=1,
+                )
+                out = lax.dot_general(
+                    dy_all[...].reshape(tokens, out_width),
+                    rhs,
+                    (((1,), (1,)), ((), ())),
+                    preferred_element_type=F32,
+                )
+                out = out.reshape(rows, cols, shard // cols, 2 * blk).astype(BF16)
+                for c in range(cols):
+                    bpart[v, c, :, :, pl.ds(n * 2 * blk, 2 * blk)] = out[:, c]
 
     def bwd_ring(v, k):
         way = 1 if v % 2 == 0 else -1
@@ -366,10 +364,11 @@
         fwd_dot(u)
         pair_copy(u).start()
 
-    def bwd_first(v):
-        bwd_dot(v)
-        bwd_ring(v, 0).start()
-        bwd_ring(v, 1).start()
+    def bwd_first(p):
+        bwd_dot(p)
+        for v in range(p * BWD_DOT, (p + 1) * BWD_DOT):
+            bwd_ring(v, 0).start()
+            bwd_ring(v, 1).start()
 
     fwd_first(0)
     fwd_first(1)
@@ -388,15 +387,14 @@
     hand_on(gather(9, below, half, half, sibling))
     gather(3, above, 0, half, tall(-1)).wait_recv()
     hand_on(gather(10, above, 0, half, sibling))
-    fwd_pair(3)
-    fwd_pair(4)
-    fwd_pair(5)
     gather(5, far, 0, half, tall(1)).wait_recv()
     hand_on(gather(11, far, 0, half, sibling))
     gather(7, far, half, half, tall(-1)).wait_recv()
     hand_on(gather(12, far, half, half, sibling))
     fwd_mid(0)
+    fwd_pair(3)
     fwd_mid(1)
+    fwd_pair(4)
     gather(4, row + twin, 0, out_width, sibling).wait_recv()
     gather(6, below + twin, 0, half, sibling).wait_recv()
     gather(8, above + twin, half, half, sibling).wait_recv()
@@ -405,31 +403,29 @@
     gather(11, far + twin, 0, half, sibling).wait_recv()
     gather(12, far + twin, half, half, sibling).wait_recv()
     bwd_first(0)
+    bwd_first(1)
+    bwd_first(2)
     fwd_mid(2)
-    bwd_first(1)
+    fwd_pair(5)
+    bwd_mid(0)
     fwd_mid(3)
-    bwd_first(2)
     fwd_mid(4)
-    bwd_first(3)
-    bwd_first(4)
-    fwd_mid(5)
-    bwd_first(5)
-    bwd_mid(0)
     fwd_end(0)
     fwd_end(1)
+    bwd_mid(1)
+    bwd_mid(2)
+    bwd_mid(3)
     fwd_end(2)
-    bwd_mid(1)
+    bwd_mid(4)
+    fwd_mid(5)
+    bwd_mid(5)
     fwd_end(3)
     fwd_end(4)
-    bwd_mid(2)
-    bwd_mid(3)
-    fwd_end(5)
-    bwd_mid(4)
-    bwd_mid(5)
     bwd_end(0)
     bwd_end(1)
     bwd_end(2)
     bwd_end(3)
+    fwd_end(5)
     bwd_end(4)
     bwd_end(5)
 

time: 39.2 us -> 37.5 us (0.957)
  Pallas kernels: 36.9 us -> 35.3 us
    pallas_call x1, Pallas kernels: 36.9 us -> 35.3 us  [local(): pl.pallas_call(functools.partial(kernel, (sections, rows, cols, block_row...]
where the time goes in v3:
time: 37.5 us; the launch traced here: 37.4 us
  Pallas kernels  35.3 us (94%)
  between operations  1.29 us (3%)
  other arithmetic  0.78 us (2%)
    pallas_call x1, Pallas kernels, local(): pl.pallas_call(functools.partial(kernel, (sections, rows, cols, block_row...  35.3 us
    select_n x1, other arithmetic, local(): dx_section = jnp.where(section >= 0, dx_raw, jnp.zeros_like(dx_raw))  0.78 us

profile of v3, /device:TPU:1, one launch (start us, length us, event | category | flops | bytes accessed | tf_op | source)
XLA Modules:
  0.0 37.4 jit_solution(12225088111747563084)
XLA Ops:
  1.3 35.3 %shard_map.95 = (bf16[8,12288]{1,0:T(8,128)(2,1)S(1)}, bf16[8,12288]{1,0:T(8,128)(2,1)S(1)}) custom-call(s32[1,1,1]{2,1,0:T(1,128)S(6)} %copy.10.count_ref, s32[1,2]{1,0:T(1,128)} %tok_hbm.1, s32[1,64]{1,0:T(1,128)} %owner_hbm.1, s32[1,115]{1,0:T(1,128)} %bitcast.4, s32[1,115]{1,0:T(1,128)} %bitcast.5, bf16[256,1536]{1,0:T(8,128)(2,1)} %x_hbm.1, ...), custom_call_target="tpu_custom_call" | custom-call | tf_op jit(solution)/shard_map/pallas_call | solution.py:490
  36.6 0.8 %broadcast_select_fusion = (bf16[8,12288]{1,0:T(8,128)(2,1)}, bf16[8,12288]{1,0:T(8,128)(2,1)}) fusion(bf16[8,12288]{1,0:T(8,128)(2,1)S(1)} %get-tuple-element.5, pred[]{:T(512)S(6)} %ge.3, bf16[8,12288]{1,0:T(8,128)(2,1)S(1)} %get-tuple-element.4, pred[]{:T(512)S(6)} %gt.3), kind=kLoop, calls=%fused_computation | loop fusion | flops 196608 | bytes 786434 | tf_op jit(solution)/shard_map/jit(_where)/select_n | solution.py:556

commit v4 on v3

--- a/solution.py
+++ b/solution.py
@@ -63,6 +63,7 @@
     bring_recv,
     bfin_send,
     dx_recv,
+    ready,
 ):
     sections, rows, cols, block_rows, block_cols = sizes
     blk = w.shape[1]
@@ -123,17 +124,22 @@
     greet(wide(1))
     greet(wide(-1))
 
-    @pl.when(sec > 0)
+    @pl.when(sec == 1)
     def _():
         for c in range(cols):
-            greet((sec - 1, row, c))
-
-
-    @pl.when(sec < sections - 1)
+            greet((0, row, c))
+
+    @pl.when(jnp.logical_and(sec > 0, sec < sections - 1))
+    def _():
+        for c in range(cols):
+            greet((sec + 1, row, c))
+
+
+    @pl.when(sec != 1)
     def _():
         pl.semaphore_wait(barrier, rows + 1 + cols)
 
-    @pl.when(sec == sections - 1)
+    @pl.when(sec == 1)
     def _():
         pl.semaphore_wait(barrier, rows + 1)
 
@@ -167,6 +173,11 @@
         for copy in copies:
             copy.start()
             gathers.append(copy)
+
+    @pl.when(sec > 1)
+    def _():
+        for c in range(cols):
+            pl.semaphore_signal(ready, inc=1, device_id=(sec - 1, row, c), device_id_type=MESH)
 
     for copy in small:
         copy.wait()
@@ -410,6 +421,11 @@
     bwd_mid(0)
     fwd_mid(3)
     fwd_mid(4)
+
+    @pl.when(jnp.logical_and(sec > 0, sec < sections - 1))
+    def _():
+        pl.semaphore_wait(ready, cols)
+
     fwd_end(0)
     fwd_end(1)
     bwd_mid(1)
@@ -532,6 +548,7 @@
             dma((BWD_UNITS, 3)),
             dma((BWD_UNITS // BWD_GROUP, rows)),
             dma,
+            pltpu.SemaphoreType.REGULAR,
         ],
         compiler_params=pltpu.CompilerParams(
             collective_id=0, has_side_effects=True, vmem_limit_bytes=32 * 1024 * 1024

time: 37.5 us -> 37.5 us (level)
  no operation moved by 1% of the time
where the time goes in v4:
time: 37.5 us; the launch traced here: 37.4 us
  Pallas kernels  35.3 us (94%)
  between operations  1.29 us (3%)
  other arithmetic  0.78 us (2%)
    pallas_call x1, Pallas kernels, local(): pl.pallas_call(functools.partial(kernel, (sections, rows, cols, block_row...  35.3 us
    select_n x1, other arithmetic, local(): dx_section = jnp.where(section >= 0, dx_raw, jnp.zeros_like(dx_raw))  0.78 us

profile of v4, /device:TPU:1, one launch (start us, length us, event | category | flops | bytes accessed | tf_op | source)
XLA Modules:
  0.0 37.4 jit_solution(5433054279170534892)
XLA Ops:
  1.3 35.3 %shard_map.95 = (bf16[8,12288]{1,0:T(8,128)(2,1)S(1)}, bf16[8,12288]{1,0:T(8,128)(2,1)S(1)}) custom-call(s32[1,1,1]{2,1,0:T(1,128)S(6)} %copy.10.count_ref, s32[1,2]{1,0:T(1,128)} %tok_hbm.1, s32[1,64]{1,0:T(1,128)} %owner_hbm.1, s32[1,115]{1,0:T(1,128)} %bitcast.4, s32[1,115]{1,0:T(1,128)} %bitcast.5, bf16[256,1536]{1,0:T(8,128)(2,1)} %x_hbm.1, ...), custom_call_target="tpu_custom_call" | custom-call | tf_op jit(solution)/shard_map/pallas_call | solution.py:506
  36.6 0.8 %broadcast_select_fusion = (bf16[8,12288]{1,0:T(8,128)(2,1)}, bf16[8,12288]{1,0:T(8,128)(2,1)}) fusion(bf16[8,12288]{1,0:T(8,128)(2,1)S(1)} %get-tuple-element.5, pred[]{:T(512)S(6)} %ge.3, bf16[8,12288]{1,0:T(8,128)(2,1)S(1)} %get-tuple-element.4, pred[]{:T(512)S(6)} %gt.3), kind=kLoop, calls=%fused_computation | loop fusion | flops 196608 | bytes 786434 | tf_op jit(solution)/shard_map/jit(_where)/select_n | solution.py:573

commit v5 on v4

--- a/solution.py
+++ b/solution.py
@@ -14,6 +14,8 @@
 BWD_UNITS = 6
 BWD_GROUP = 1
 BWD_DOT = 2
+FAR_UNITS = 2
+NEAR = 6
 
 
 def kernel(
@@ -50,6 +52,9 @@
     bwd_direct,
     bwd_comb,
     bwd_fin,
+    fpart,
+    far_in,
+    far_fin,
     load_sem,
     gather_send,
     gather_recv,
@@ -62,6 +67,8 @@
     bring_send,
     bring_recv,
     bfin_send,
+    far_send,
+    far_recv,
     dx_recv,
     ready,
 ):
@@ -96,7 +103,7 @@
 
     load_w = pltpu.make_async_copy(w_hbm, w.at[pl.ds(0, slot_total)], load_sem.at[0])
     load_x = pltpu.make_async_copy(x_hbm, x, load_sem.at[1])
-    load_dy = pltpu.make_async_copy(dy_hbm, dy_all.at[row], load_sem.at[2])
+    load_dy = pltpu.make_async_copy(dy_hbm, dy_all.at[core], load_sem.at[2])
     load_dy.start()
     small = [
         pltpu.make_async_copy(there, here, load_sem.at[4 + k])
@@ -143,11 +150,12 @@
     def _():
         pl.semaphore_wait(barrier, rows + 1)
 
-    def gather(k, src_row, lo, width, device):
-        place = dy_all.at[src_row, :, pl.ds(lo, width)]
-        return pltpu.make_async_remote_copy(
-            src_ref=place,
-            dst_ref=place,
+    OWN, ABOVE, BELOW, FAR = 0, 2, 4, 6
+
+    def gather(k, held, there, lo, width, device):
+        return pltpu.make_async_remote_copy(
+            src_ref=dy_all.at[held, :, pl.ds(lo, width)],
+            dst_ref=dy_all.at[there, :, pl.ds(lo, width)],
             send_sem=gather_send.at[k],
             recv_sem=gather_recv.at[k],
             device_id=device,
@@ -155,16 +163,23 @@
         )
 
     half = out_width // 2
-    below, above, far = high(-1) * 2 + core, high(1) * 2 + core, high(2) * 2 + core
-    twin = 1 - 2 * core
+
+    def arrived(k, held, lo, width):
+        gather(k, held + core, held + core, lo, width, sibling).wait_recv()
+
+    def crossed(k, held, lo, width):
+        gather(k, held + 1 - core, held + 1 - core, lo, width, sibling).wait_recv()
+
+    def relay(k, held, lo, width):
+        return gather(k, held + core, held + core, lo, width, sibling)
 
     load_dy.wait()
     gathers = [
-        gather(0, row, 0, half, tall(1)),
-        gather(1, row, half, half, tall(-1)),
-        gather(2, row, half, half, tall(1)),
-        gather(3, row, 0, half, tall(-1)),
-        gather(4, row, 0, out_width, sibling),
+        gather(0, core, BELOW + core, 0, half, tall(1)),
+        gather(1, core, ABOVE + core, half, half, tall(-1)),
+        gather(2, core, BELOW + core, half, half, tall(1)),
+        gather(3, core, ABOVE + core, 0, half, tall(-1)),
+        relay(4, OWN, 0, out_width),
     ]
     for copy in gathers:
         copy.start()
@@ -296,28 +311,54 @@
             for c in range(cols):
                 y_copy(u, c).start()
 
+    def bwd_tile(first, lo, hi):
+        rhs = jnp.concatenate(
+            [
+                jnp.concatenate(
+                    [w[slot_ref[0, (first + j) * block_cols + c]] for j in range(2)], axis=0
+                )
+                for c in range(block_cols)
+            ],
+            axis=1,
+        )
+        out = lax.dot_general(
+            dy_all[lo:hi].reshape((hi - lo) * shard, out_width),
+            rhs,
+            (((1,), (1,)), ((), ())),
+            preferred_element_type=F32,
+        )
+        return out.reshape(hi - lo, cols, shard // cols, 2 * blk).astype(BF16)
+
     def bwd_dot(p):
         for v in range(p * BWD_DOT, (p + 1) * BWD_DOT):
             for n in range(bwd_width // (2 * blk)):
-                first = (v * (bwd_width // (2 * blk)) + n) * 2
-                rhs = jnp.concatenate(
-                    [
-                        jnp.concatenate(
-                            [w[slot_ref[0, (first + j) * block_cols + c]] for j in range(2)], axis=0
-                        )
-                        for c in range(block_cols)
-                    ],
-                    axis=1,
-                )
-                out = lax.dot_general(
-                    dy_all[...].reshape(tokens, out_width),
-                    rhs,
-                    (((1,), (1,)), ((), ())),
-                    preferred_element_type=F32,
-                )
-                out = out.reshape(rows, cols, shard // cols, 2 * blk).astype(BF16)
+                out = bwd_tile((v * (bwd_width // (2 * blk)) + n) * 2, 0, NEAR)
                 for c in range(cols):
                     bpart[v, c, :, :, pl.ds(n * 2 * blk, 2 * blk)] = out[:, c]
+
+    far_width = in_width // FAR_UNITS
+
+    def far_copy(g, by):
+        return pltpu.make_async_remote_copy(
+            src_ref=fpart.at[g, across(by)],
+            dst_ref=far_in.at[g, by - 1],
+            send_sem=far_send.at[g, by - 1],
+            recv_sem=far_recv.at[g, by - 1],
+            device_id=wide(by),
+            device_id_type=MESH,
+        )
+
+    def far_first(g):
+        def tile(n, carry):
+            out = bwd_tile((g * (far_width // (2 * blk)) + n) * 2, NEAR, rows)
+            at = pl.ds(pl.multiple_of(n * 2 * blk, 2 * blk), 2 * blk)
+            for c in range(cols):
+                fpart[g, c, :, :, at] = out[:, c]
+            return carry
+
+        lax.fori_loop(0, far_width // (2 * blk), tile, 0, unroll=True)
+        for by in (2, 1, 3):
+            far_copy(g, by).start()
 
     def bwd_ring(v, k):
         way = 1 if v % 2 == 0 else -1
@@ -340,36 +381,73 @@
 
     group_width = BWD_GROUP * bwd_width
 
-    def dx_at(g):
-        return dx_out.at[:, pl.ds(pl.multiple_of(row * in_width + g * group_width, 128), group_width)]
-
-    def dx_copy(g, by):
-        to = lax.rem(row + by, rows)
-        return pltpu.make_async_remote_copy(
-            src_ref=bwd_fin.at[g, to],
-            dst_ref=dx_at(g),
-            send_sem=bfin_send.at[g, by],
+    def home(q):
+        return high((0, 1, -1, 2)[q // 2]) * 2 + q % 2
+
+    def kept(q, total):
+        token = home(q) * shard + col * (shard // cols) + lax.broadcasted_iota(jnp.int32, total.shape, 0)
+        return jnp.where(token < tok_ref[0, 1], total, 0.0).astype(BF16)
+
+    def dx_at(lo, width):
+        return dx_out.at[:, pl.ds(pl.multiple_of(row * in_width + lo, 128), width)]
+
+    def dx_copy(g, q):
+        return pltpu.make_async_remote_copy(
+            src_ref=bwd_fin.at[g, q],
+            dst_ref=dx_at(g * group_width, group_width),
+            send_sem=bfin_send.at[g, q],
             recv_sem=dx_recv,
-            device_id=(sec, to, col),
+            device_id=(sec, home(q), col),
+            device_id_type=MESH,
+        )
+
+    def dx_sibling(g):
+        return pltpu.make_async_remote_copy(
+            src_ref=bwd_fin.at[g, 1 - core],
+            dst_ref=dx_at(g * group_width, group_width),
+            send_sem=bfin_send.at[g, 1],
+            recv_sem=dx_recv,
+            device_id=sibling,
             device_id_type=MESH,
         )
 
     def dx_own(g):
-        return pltpu.make_async_copy(bwd_fin.at[g, row], dx_at(g), bfin_send.at[g, 0])
+        return pltpu.make_async_copy(
+            bwd_fin.at[g, core], dx_at(g * group_width, group_width), bfin_send.at[g, 0]
+        )
+
+    def dx_far(g, k):
+        return pltpu.make_async_remote_copy(
+            src_ref=far_fin.at[g, k],
+            dst_ref=dx_at(g * far_width, far_width),
+            send_sem=far_send.at[g, 3 + k],
+            recv_sem=dx_recv,
+            device_id=(sec, home(NEAR + k), col),
+            device_id_type=MESH,
+        )
 
     def bwd_end(v):
         bwd_ring(v, 1).wait_recv()
         bwd_ring(v, 2).wait_recv()
         total = bpart[v, col].astype(F32) + bwd_direct[v].astype(F32) + bwd_comb[v].astype(F32)
-        token = lax.broadcasted_iota(jnp.int32, total.shape, 0) * shard + col * (shard // cols)
-        token = token + lax.broadcasted_iota(jnp.int32, total.shape, 1)
-        total = jnp.where(token < tok_ref[0, 1], total, 0.0).astype(BF16)
         g = v // BWD_GROUP
-        bwd_fin[g, :, :, pl.ds((v % BWD_GROUP) * bwd_width, bwd_width)] = total
+        at = pl.ds((v % BWD_GROUP) * bwd_width, bwd_width)
+        for q in range(NEAR):
+            bwd_fin[g, q, :, at] = kept(q, total[q])
         if v % BWD_GROUP == BWD_GROUP - 1:
-            for by in range(1, rows):
-                dx_copy(g, by).start()
+            for q in range(2, NEAR):
+                dx_copy(g, q).start()
+            dx_sibling(g).start()
             dx_own(g).start()
+
+    def far_end(g):
+        total = fpart[g, col].astype(F32)
+        for by in (1, 2, 3):
+            far_copy(g, by).wait_recv()
+            total = total + far_in[g, by - 1].astype(F32)
+        for k in range(2):
+            far_fin[g, k] = kept(NEAR + k, total[k])
+            dx_far(g, k).start()
 
     def fwd_first(u):
         fwd_dot(u)
@@ -385,42 +463,46 @@
     fwd_first(1)
     fwd_first(2)
     fwd_first(3)
-    gather(0, below, 0, half, tall(1)).wait_recv()
-    hand_on(gather(5, below, 0, half, tall(1)), gather(6, below, 0, half, sibling))
-    gather(1, above, half, half, tall(-1)).wait_recv()
-    hand_on(gather(7, above, half, half, tall(-1)), gather(8, above, half, half, sibling))
+    arrived(0, BELOW, 0, half)
+    hand_on(gather(5, BELOW + core, FAR + core, 0, half, tall(1)), relay(6, BELOW, 0, half))
+    arrived(1, ABOVE, half, half)
+    hand_on(gather(7, ABOVE + core, FAR + core, half, half, tall(-1)), relay(8, ABOVE, half, half))
     fwd_pair(0)
     fwd_pair(1)
     fwd_first(4)
     fwd_pair(2)
     fwd_first(5)
-    gather(2, below, half, half, tall(1)).wait_recv()
-    hand_on(gather(9, below, half, half, sibling))
-    gather(3, above, 0, half, tall(-1)).wait_recv()
-    hand_on(gather(10, above, 0, half, sibling))
-    gather(5, far, 0, half, tall(1)).wait_recv()
-    hand_on(gather(11, far, 0, half, sibling))
-    gather(7, far, half, half, tall(-1)).wait_recv()
-    hand_on(gather(12, far, half, half, sibling))
+    arrived(2, BELOW, half, half)
+    hand_on(relay(9, BELOW, half, half))
+    arrived(3, ABOVE, 0, half)
+    hand_on(relay(10, ABOVE, 0, half))
+    fwd_pair(3)
+    fwd_pair(4)
+    fwd_pair(5)
+    crossed(4, OWN, 0, out_width)
+    crossed(6, BELOW, 0, half)
+    crossed(8, ABOVE, half, half)
+    crossed(9, BELOW, half, half)
+    crossed(10, ABOVE, 0, half)
+    bwd_first(0)
+    arrived(5, FAR, 0, half)
+    hand_on(relay(11, FAR, 0, half))
+    arrived(7, FAR, half, half)
+    hand_on(relay(12, FAR, half, half))
     fwd_mid(0)
-    fwd_pair(3)
+    bwd_first(1)
     fwd_mid(1)
-    fwd_pair(4)
-    gather(4, row + twin, 0, out_width, sibling).wait_recv()
-    gather(6, below + twin, 0, half, sibling).wait_recv()
-    gather(8, above + twin, half, half, sibling).wait_recv()
-    gather(9, below + twin, half, half, sibling).wait_recv()
-    gather(10, above + twin, 0, half, sibling).wait_recv()
-    gather(11, far + twin, 0, half, sibling).wait_recv()
-    gather(12, far + twin, half, half, sibling).wait_recv()
-    bwd_first(0)
-    bwd_first(1)
+    fwd_mid(2)
+    fwd_mid(3)
     bwd_first(2)
-    fwd_mid(2)
-    fwd_pair(5)
     bwd_mid(0)
-    fwd_mid(3)
+    bwd_mid(1)
     fwd_mid(4)
+    fwd_mid(5)
+    crossed(11, FAR, 0, half)
+    crossed(12, FAR, half, half)
+    far_first(0)
+    bwd_mid(2)
 
     @pl.when(jnp.logical_and(sec > 0, sec < sections - 1))
     def _():
@@ -428,20 +510,20 @@
 
     fwd_end(0)
     fwd_end(1)
-    bwd_mid(1)
-    bwd_mid(2)
     bwd_mid(3)
     fwd_end(2)
+    far_first(1)
     bwd_mid(4)
-    fwd_mid(5)
-    bwd_mid(5)
     fwd_end(3)
     fwd_end(4)
+    bwd_mid(5)
+    fwd_end(5)
     bwd_end(0)
     bwd_end(1)
     bwd_end(2)
+    far_end(0)
     bwd_end(3)
-    fwd_end(5)
+    far_end(1)
     bwd_end(4)
     bwd_end(5)
 
@@ -455,9 +537,15 @@
         for k in range(3):
             bwd_ring(v, k).wait_send()
     for g in range(BWD_UNITS // BWD_GROUP):
-        for by in range(1, rows):
-            dx_copy(g, by).wait_send()
+        for q in range(2, NEAR):
+            dx_copy(g, q).wait_send()
+        dx_sibling(g).wait_send()
         dx_own(g).wait()
+    for g in range(FAR_UNITS):
+        for by in (1, 2, 3):
+            far_copy(g, by).wait_send()
+        for k in range(2):
+            dx_far(g, k).wait_send()
 
     @pl.when(sec < sections - 1)
     def _():
@@ -501,6 +589,7 @@
     owned = tokens // (rows * cols)
     fwd_width = out_width // FWD_UNITS
     bwd_width = in_width // BWD_UNITS
+    far_width = in_width // FAR_UNITS
 
     dma = pltpu.SemaphoreType.DMA
     y_raw, dx_raw = pl.pallas_call(
@@ -530,11 +619,14 @@
             pltpu.VMEM((FWD_UNITS, shard, fwd_width), BF16),
             pltpu.VMEM((FWD_UNITS, shard, fwd_width), BF16),
             pltpu.VMEM((FWD_UNITS, cols, owned, fwd_width), BF16),
-            pltpu.VMEM((BWD_UNITS, cols, rows, owned, bwd_width), BF16),
-            pltpu.VMEM((BWD_UNITS, rows, owned, bwd_width), BF16),
-            pltpu.VMEM((BWD_UNITS, rows, owned, bwd_width), BF16),
-            pltpu.VMEM((BWD_UNITS, rows, owned, bwd_width), BF16),
-            pltpu.VMEM((BWD_UNITS // BWD_GROUP, rows, owned, BWD_GROUP * bwd_width), BF16),
+            pltpu.VMEM((BWD_UNITS, cols, NEAR, owned, bwd_width), BF16),
+            pltpu.VMEM((BWD_UNITS, NEAR, owned, bwd_width), BF16),
+            pltpu.VMEM((BWD_UNITS, NEAR, owned, bwd_width), BF16),
+            pltpu.VMEM((BWD_UNITS, NEAR, owned, bwd_width), BF16),
+            pltpu.VMEM((BWD_UNITS // BWD_GROUP, NEAR, owned, BWD_GROUP * bwd_width), BF16),
+            pltpu.VMEM((FAR_UNITS, cols, rows - NEAR, owned, far_width), BF16),
+            pltpu.VMEM((FAR_UNITS, cols - 1, rows - NEAR, owned, far_width), BF16),
+            pltpu.VMEM((FAR_UNITS, rows - NEAR, owned, far_width), BF16),
             dma((8,)),
             dma((13,)),
             dma((13,)),
@@ -546,7 +638,9 @@
             dma,
             dma((BWD_UNITS, 3)),
             dma((BWD_UNITS, 3)),
-            dma((BWD_UNITS // BWD_GROUP, rows)),
+            dma((BWD_UNITS // BWD_GROUP, NEAR)),
+            dma((FAR_UNITS, 5)),
+            dma((FAR_UNITS, 3)),
             dma,
             pltpu.SemaphoreType.REGULAR,
         ],

time: 37.5 us -> 37.3 us (level)
  no operation moved by 1% of the time
where the time goes in v5:
time: 37.3 us; the launch traced here: 37.2 us
  Pallas kernels  35.1 us (94%)
  between operations  1.29 us (3%)
  other arithmetic  0.78 us (2%)
    pallas_call x1, Pallas kernels, local(): pl.pallas_call(functools.partial(kernel, (sections, rows, cols, block_row...  35.1 us
    select_n x1, other arithmetic, local(): dx_section = jnp.where(section >= 0, dx_raw, jnp.zeros_like(dx_raw))  0.78 us

profile of v5, /device:TPU:1, one launch (start us, length us, event | category | flops | bytes accessed | tf_op | source)
XLA Modules:
  0.0 37.2 jit_solution(10541565351672375750)
XLA Ops:
  1.3 35.1 %shard_map.95 = (bf16[8,12288]{1,0:T(8,128)(2,1)S(1)}, bf16[8,12288]{1,0:T(8,128)(2,1)S(1)}) custom-call(s32[1,1,1]{2,1,0:T(1,128)S(6)} %copy.10.count_ref, s32[1,2]{1,0:T(1,128)} %tok_hbm.1, s32[1,64]{1,0:T(1,128)} %owner_hbm.1, s32[1,115]{1,0:T(1,128)} %bitcast.4, s32[1,115]{1,0:T(1,128)} %bitcast.5, bf16[256,1536]{1,0:T(8,128)(2,1)} %x_hbm.1, ...), custom_call_target="tpu_custom_call" | custom-call | tf_op jit(solution)/shard_map/pallas_call | solution.py:595
  36.4 0.8 %broadcast_select_fusion = (bf16[8,12288]{1,0:T(8,128)(2,1)}, bf16[8,12288]{1,0:T(8,128)(2,1)}) fusion(bf16[8,12288]{1,0:T(8,128)(2,1)S(1)} %get-tuple-element.5, pred[]{:T(512)S(6)} %ge.3, bf16[8,12288]{1,0:T(8,128)(2,1)S(1)} %get-tuple-element.4, pred[]{:T(512)S(6)} %gt.3), kind=kLoop, calls=%fused_computation | loop fusion | flops 196608 | bytes 786434 | tf_op jit(solution)/shard_map/jit(_where)/select_n | solution.py:667
